TPU v7x, 32 devices: a whole 2x2x4 slice. The times are simulated.
32 devices in a mesh: lat: 16 (over z, y, core), ma: 2 (over x).
Axes of the slice: x: 2, y: 2, z: 4, core: 2. Of those that a mesh axis runs over, the one named last changes fastest.
Arguments:
- spectral: bfloat16 [16, 2, 648, 768], P('ma'), may hold values from -0.25 to 0.25
- set_pair: int32 [16], P('ma'), may hold values from 0 to 639, as said below
- lat_sines: float32 [640], replicated, may hold values from 0.005 to 0.3
Outputs:
- grid: bfloat16 [1280, 16, 2, 768], P(('lat', 'ma'))
Inputs may be any that keep to these rules, and one draw needn't show every extreme that they name: `set_pair`: the values are distinct; 0 and 639 both occur.
All inputs are finite; a program needn't handle non-finite values.
Results may differ from a plain program's by a relative error of at most 0.0058.
Values may be sent and summed in bfloat16 or wider, within the bound.
No kernel may reach another device: no remote copies, remote signals or barrier semaphores. Data moves between devices by JAX's collectives and lax.ppermute only.
A program may use at most 128 MiB of HBM per device.

v0:
```python
import jax
import jax.numpy as jnp
from jax import lax
from jax.sharding import PartitionSpec as P

M = 1280
NH = 648
BAND = 80


def legendre_runs(sines, pairs):
    span_size = 128
    block_count = (M + 1 + span_size - 1) // span_size
    padded_length = block_count * span_size
    set_count = pairs.shape[0]
    positions = jnp.arange(padded_length, dtype=jnp.int32)[None, :]
    run_length = (M - pairs)[:, None]
    first_run = positions < run_length
    inside = positions <= M
    order_m = jnp.where(first_run, pairs[:, None], M - 1 - pairs[:, None]).astype(jnp.float32)
    offset_k = jnp.where(first_run, positions, positions - run_length).astype(jnp.float32)
    degree = order_m + offset_k
    recurring = offset_k > 0.5
    beyond_one = offset_k > 1.5
    prior_degree = degree - 1.0
    factor_a = jnp.sqrt(
        jnp.where(recurring, 4.0 * degree * degree - 1.0, 1.0)
        / jnp.where(recurring, degree * degree - order_m * order_m, 1.0)
    )
    factor_b = jnp.sqrt(
        jnp.where(beyond_one, prior_degree * prior_degree - order_m * order_m, 0.0)
        / jnp.where(beyond_one, 4.0 * prior_degree * prior_degree - 1.0, 1.0)
    )
    log_start = 0.5 * (
        lax.lgamma(order_m + 1.5)
        - lax.lgamma(order_m + 1.0)
        - lax.lgamma(jnp.ones_like(order_m) * 1.5)
    ) + 0.5 * jnp.log(jnp.ones_like(order_m) * 0.5)
    factor_now = jnp.where(recurring & inside, factor_a, 0.0)
    factor_back = jnp.where(recurring & inside, -(factor_a * factor_b), 0.0)
    seed_mask = jnp.where(jnp.logical_not(recurring) & inside, 1.0, 0.0).astype(jnp.float32)
    log_cosine = jnp.log(1.0 - sines * sines)

    def to_blocks(table):
        return table.reshape(set_count, block_count, span_size).transpose(1, 0, 2)

    block_tables = (
        to_blocks(factor_now),
        to_blocks(factor_back),
        to_blocks(log_start),
        to_blocks(order_m),
        to_blocks(seed_mask),
    )

    def advance(carry, block_data):
        latest, earlier_value = carry
        now_table, back_table, start_table, order_table, mask_table = block_data
        produced = []
        for column in range(span_size):
            seed_value = mask_table[:, column : column + 1] * jnp.exp(
                start_table[:, column : column + 1]
                + 0.5 * order_table[:, column : column + 1] * log_cosine[None, :]
            )
            current = (
                now_table[:, column : column + 1] * sines[None, :] * latest
                + back_table[:, column : column + 1] * earlier_value
                + seed_value
            )
            earlier_value = latest
            latest = current
            produced.append(current)
        return ((latest, earlier_value), jnp.stack(produced, axis=2))

    zero_state = jnp.zeros((set_count, sines.shape[0]), jnp.float32)
    _, blocks_out = lax.scan(advance, (zero_state, zero_state), block_tables)
    result = blocks_out.transpose(1, 2, 0, 3).reshape(set_count, sines.shape[0], padded_length)
    return result[:, :, : M + 1]


def parity_weights(values, pairs, parity):
    slot_index = jnp.arange(NH, dtype=jnp.int32)[None, :]
    run_length = (M - pairs)[:, None]
    first_count = (run_length + 1 - parity) // 2
    second_count = (pairs[:, None] + 2 - parity) // 2
    source = jnp.where(
        slot_index < first_count,
        2 * slot_index + parity,
        run_length + 2 * (slot_index - first_count) + parity,
    )
    source = jnp.clip(source, 0, M)
    picked = jnp.take_along_axis(values, source[:, None, :], axis=2)
    in_first = (slot_index < first_count)[:, None, :]
    in_second = ((slot_index >= first_count) & (slot_index < first_count + second_count))[
        :, None, :
    ]
    return jnp.stack(
        [jnp.where(in_first, picked, 0.0), jnp.where(in_second, picked, 0.0)], axis=2
    ).astype(jnp.bfloat16)


def project(weights, coeffs):
    summed = jnp.einsum("stje,sec->tsjc", weights, coeffs, preferred_element_type=jnp.float32)
    return summed.astype(jnp.bfloat16)


def local(spectral, set_pair, lat_sines):
    half_lat = lax.axis_size("lat") // 2
    lat_index = lax.axis_index("lat")
    hemisphere = lat_index // half_lat
    band_index = lat_index % half_lat
    band_sines = lax.dynamic_slice_in_dim(lat_sines, band_index * BAND, BAND)
    sign_factor = (1 - 2 * hemisphere).astype(jnp.float32)
    values = legendre_runs(band_sines, set_pair)
    even_part = project(parity_weights(values, set_pair, 0), spectral[:, 0])
    odd_part = project(parity_weights(values, set_pair, 1), spectral[:, 1])
    even_part, odd_part = lax.optimization_barrier((even_part, odd_part))
    combined = (even_part.astype(jnp.float32) + sign_factor * odd_part.astype(jnp.float32)).astype(
        jnp.bfloat16
    )
    return lax.all_to_all(combined, "ma", split_axis=0, concat_axis=1, tiled=True)


def solution(mesh):
    placed = (P("ma", None, None, None), P("ma"), P())
    return jax.shard_map(
        local,
        mesh=mesh,
        in_specs=placed,
        out_specs=P(("lat", "ma"), None, None, None),
        check_vma=False,
    )
```

profile of v0, /device:TPU:0, one launch (start us, length us, event | category | flops | bytes accessed | tf_op | source)
XLA Modules:
  0.0 313.1 jit_solution(18113006901872707660)
XLA Ops:
  0.0 0.7 fusion.206
  0.7 0.1 and_bitcast_fusion
  0.8 0.1 bitcast_or_fusion
  1.1 0.7 fusion.157
  1.9 1.3 negate_select_fusion
  3.2 0.8 subtract_log_fusion
  4.0 146.7 %while.15 = (s32[]{:T(128)}, f32[8,80]{1,0:T(8,128)S(1)}, f32[8,80]{1,0:T(8,128)S(1)}, bf16[11,8,80,128]{2,1,3,0:T(8,128)(2,1)}, f32[11,8,128]{2,1,0:T(8,128)S(1...) while((s32[]{:T(128)}, f32[8,80]{1,0:T(8,128)S(1)}, ...), condition=%wide.region_1.2_spmd.clone, body=%wide.region_0.1_spmd.clone.sunk | while | flops 658306 | bytes 3099072 | solution.py:75
  4.0 0.1 copy.67
  4.2 0.1 copy.65
  4.5 0.1 copy.69
  4.8 0.1 copy.68
  5.0 0.1 copy.66
  16.6 0.7 bitcast_dynamic-update-slice_fusion.2
  17.4 0.1 copy.67
  17.6 0.1 copy.65
  17.9 0.1 copy.69
  18.1 0.1 copy.68
  18.3 0.1 copy.66
  29.9 0.7 bitcast_dynamic-update-slice_fusion.2
  30.7 0.1 copy.67
  30.9 0.1 copy.65
  31.2 0.1 copy.69
  31.4 0.1 copy.68
  31.7 0.1 copy.66
  43.3 0.7 bitcast_dynamic-update-slice_fusion.2
  44.0 0.1 copy.67
  44.3 0.1 copy.65
  44.5 0.1 copy.69
  44.8 0.1 copy.68
  45.0 0.1 copy.66
  56.6 0.7 bitcast_dynamic-update-slice_fusion.2
  57.3 0.1 copy.67
  57.6 0.1 copy.65
  57.8 0.1 copy.69
  58.1 0.1 copy.68
  69.9 0.7 bitcast_dynamic-update-slice_fusion.2
  70.7 0.1 copy.67
  70.9 0.1 copy.65
  83.3 0.7 bitcast_dynamic-update-slice_fusion.2
  84.0 0.1 copy.67
  96.6 0.7 bitcast_dynamic-update-slice_fusion.2
  97.3 0.1 copy.67
  109.9 0.8 bitcast_dynamic-update-slice_fusion.2
  110.7 0.1 copy.67
  123.3 0.7 bitcast_dynamic-update-slice_fusion.2
  124.0 0.1 copy.67
  136.6 0.7 bitcast_dynamic-update-slice_fusion.2
  137.4 0.1 copy.67
  150.0 0.7 bitcast_dynamic-update-slice_fusion.2
  150.7 1.8 slice.3216
  152.5 56.4 %gather_fusion.1 = bf16[5184,80]{1,0:T(8,128)(2,1)} fusion(bf16[8,80,1281]{1,0,2:T(8,128)(2,1)S(1)} %slice.3216, s32[5184]{0:T(1024)S(1)} %reshape.565), kind=kCustom, calls=%fused_computation.1.clone | custom fusion | bytes 1700352 | tf_op jit(solution)/shard_map/jit(take_along_axis)/gather | solution.py:91
  208.9 56.2 %gather_fusion = bf16[5184,80]{1,0:T(8,128)(2,1)} fusion(bf16[8,80,1281]{1,0,2:T(8,128)(2,1)S(1)} %slice.3216, s32[5184]{0:T(1024)S(1)} %reshape.560), kind=kCustom, calls=%fused_computation.clone | custom fusion | bytes 1700352 | tf_op jit(solution)/shard_map/jit(take_along_axis)/gather | solution.py:91
  265.1 1.7 copy.34
  266.8 1.4 copy.38
  268.4 1.7 fusion.155
  270.1 5.1 %convert_bitcast_fusion = bf16[80,8,2,768]{3,0,2,1:T(8,128)(2,1)S(1)} fusion(bf16[8,2,648,768]{3,2,1,0:T(8,128)(2,1)} %param.7, bf16[8,80,1,648]{3,1,0,2:T(8,128)(2,1)S(1)} %get-tuple-element.1044, bf16[8,80,1,648]{3,1,0,2:T(8,128)(2,1)S(1)} %get-tuple-element.1043), kind=kOutput, calls=%fused_computation.1054 | convolution fusion | flops 1275832320 | bytes 11587584 | tf_op jit(solution)/shard_map/stje,sec->tsjc/dot_general | solution.py:102
  275.2 0.5 fusion.153
  275.8 1.2 slice-done.2
  277.0 1.0 slice-done.3
  278.0 2.1 convert_bitcast_fusion.1
  280.1 0.6 add_convert_fusion
  280.7 1.5 copy.41
  282.2 27.5 %all_to_all.18 = bf16[80,8,2,768]{3,2,1,0:T(2,128)(2,1)S(1)} all-to-all(bf16[80,8,2,768]{3,2,1,0:T(2,128)(2,1)S(1)} %copy.41), channel_id=1, replica_groups=mesh['lat'=16,'ma'=2] {'ma'}, dimensions={0} | all-to-all | bytes 3932160 | tf_op jit(solution)/shard_map/all_to_all | solution.py:120
  309.7 3.4 %copy.42 = bf16[40,2,8,2,768]{4,3,2,1,0:T(2,128)(2,1)} copy(bf16[40,2,8,2,768]{4,3,2,0,1:T(2,128)(2,1)S(1)} %bitcast.1958) | data formatting | bytes 3932160 | tf_op jit(solution)/shard_map/all_to_all | solution.py:120
  (1868 shorter events, 132.1 us)
Async XLA Ops:
  265.1 1.8 copy-start
  270.1 5.7 %slice-start = ((s8[15925248]{0:T(1024)(128)(4,1)}), s8[4194304]{0:T(1024)(128)(4,1)S(1)}, s32[]{:S(2)}) async-start(s8[15925248]{0:T(1024)(128)(4,1)} %bitcast.1997), calls=%async_computation.1 | async-start | bytes 8388608
  270.1 5.7 %slice-start.1 = ((s8[15925248]{0:T(1024)(128)(4,1)}), s8[4194304]{0:T(1024)(128)(4,1)S(1)}, s32[]{:S(2)}) async-start(s8[15925248]{0:T(1024)(128)(4,1)} %bitcast.1997), calls=%async_computation.2 | async-start | bytes 8388608
  270.1 6.9 %slice-start.2 = ((s8[15925248]{0:T(1024)(128)(4,1)}), s8[4194304]{0:T(1024)(128)(4,1)S(1)}, s32[]{:S(2)}) async-start(s8[15925248]{0:T(1024)(128)(4,1)} %bitcast.1997), calls=%async_computation.3 | async-start | bytes 8388608
  270.1 7.9 %slice-start.3 = ((s8[15925248]{0:T(1024)(128)(4,1)}), s8[3342336]{0:T(1024)(128)(4,1)S(1)}, s32[]{:S(2)}) async-start(s8[15925248]{0:T(1024)(128)(4,1)} %bitcast.1997), calls=%async_computation.4 | async-start | bytes 6684672
where the time goes:
time: 313 us
  local copies, waits for them, and re-layouts  142 us (45%)
  other arithmetic  132 us (42%)
  blocking collectives  27.5 us (9%)
  matrix products  7.22 us (2%)
  loops' own time  3.68 us (1%)
    while x1397, other arithmetic  123 us
    gather x6, local copies, waits for them, and re-layouts, parity_weights(): picked = jnp.take_along_axis(values, source[:, None, :], axis=2)  116 us
    all_to_all x1, blocking collectives, local(): lax.all_to_all(combined, 'ma', split_axis=0, concat_axis=1, tiled=True)  27.5 us
    dynamic_update_slice x11, local copies, waits for them, and re-layouts, legendre_runs(): _, blocks_out = lax.scan(advance, (zero_state, zero_state), block_tables)  8.07 us
    dot_general x2, matrix products, project(): jnp.einsum('stje,sec->tsjc', weights, coeffs, preferred_element_type=jnp....  7.22 us

commit v1 on v0

v1 whole, which is shorter than its diff:
```python
import functools

import jax
import jax.numpy as jnp
from jax import lax
from jax.experimental import pallas as pl
from jax.experimental.pallas import tpu as pltpu
from jax.sharding import PartitionSpec as P

M = 1280
LANES = 128
F32 = jnp.float32
BF16 = jnp.bfloat16
CHUNKS = (2, 2, 2, 2)
VMEM = pl.BlockSpec(memory_space=pltpu.VMEM)
SMEM = pl.BlockSpec(memory_space=pltpu.SMEM)
ANY = pl.BlockSpec(memory_space=pl.ANY)
PARAMS = pltpu.CompilerParams(vmem_limit_bytes=48 << 20)


def start_sum(order):
    total = jnp.zeros((order.shape[0], LANES), F32)
    for block in range(M // LANES):
        k = lax.broadcasted_iota(jnp.int32, total.shape, 1) + (block * LANES + 1)
        total = total + jnp.where(k <= order, jnp.log(1.0 + 0.5 / k.astype(F32)), 0.0)
    return jnp.sum(total, axis=1, keepdims=True)


def coefficients(slot, parity, pair, first_count, count):
    first = slot < first_count
    order = jnp.where(first, pair, M - 1 - pair)
    offset = jnp.where(first, 2 * slot, 2 * (slot - first_count)) + parity
    valid = (offset >= 2) & (slot < count)
    degree = (order + offset).astype(F32)
    square = order.astype(F32) * order.astype(F32)

    def parts(k):
        return k * k - square, 4.0 * k * k - 1.0

    (u0, d0), (u1, d1), (u2, d2), (u3, d3) = (parts(degree - back) for back in range(4))
    u0 = jnp.where(valid, u0, 1.0)
    u1 = jnp.where(valid, u1, 1.0)
    a = jnp.sqrt((d1 / u1) * (d0 / u0))
    b = u1 / d1 + u2 / d2
    g = a * jnp.sqrt(jnp.maximum((u2 / d2) * (u3 / d3), 0.0))
    a, ab, g = (jnp.where(valid, value, 0.0) for value in (a, a * b, g))
    return a, ab, jnp.where(slot == 0, -1.0, g)


def legendre(pair_ref, sign_ref, x_ref, tab_ref, coef_ref, p_ref, pt_ref, sets, slots):
    rows = 2 * sets
    low = LANES // rows
    high = x_ref.shape[0]
    blocks = -(-slots // LANES)
    sub = lax.broadcasted_iota(jnp.int32, (rows, 1), 0)
    pair = jnp.zeros((rows, 1), jnp.int32)
    for s in range(sets):
        pair = jnp.where(sub % sets == s, pair_ref[s], pair)
    parity = sub // sets
    first_count = (M - pair + 1 - parity) // 2
    count = first_count + (pair + 2 - parity) // 2
    for block in range(blocks):
        slot = lax.broadcasted_iota(jnp.int32, (rows, LANES), 1) + block * LANES
        for c, table in enumerate(coefficients(slot, parity, pair, first_count, count)):
            tab_ref[pl.ds(c * rows, rows), pl.ds(block * LANES, LANES)] = table
    for c in range(3):
        for block in range(blocks):
            wide = jnp.concatenate(
                [
                    jnp.broadcast_to(tab_ref[pl.ds(c * rows + r, 1), pl.ds(block * LANES, LANES)], (low, LANES))
                    for r in range(rows)
                ],
                axis=0,
            )
            coef_ref[c, pl.ds(block * LANES, LANES), :] = wide.T
    def spread(column):
        return jnp.broadcast_to(
            jnp.concatenate([jnp.broadcast_to(column[r : r + 1], (low, LANES)) for r in range(rows)], axis=0).T[:1],
            (1, LANES),
        )

    order1 = pair
    order2 = M - 1 - pair
    logs1 = spread(start_sum(order1))
    logs2 = spread(start_sum(order2))
    lane_qs = lax.broadcasted_iota(jnp.int32, (1, LANES), 1) // low
    pair_lane = jnp.zeros((1, LANES), jnp.int32)
    for s in range(sets):
        pair_lane = jnp.where(lane_qs % sets == s, pair_ref[s], pair_lane)
    odd = lane_qs >= sets
    parity_lane = odd.astype(jnp.int32)
    first_lane = (M - pair_lane + 1 - parity_lane) // 2
    x = x_ref[...]
    x2 = x * x
    log_cos = jnp.log(1.0 - x2)
    sign = sign_ref[0]

    def seed(order, logs):
        m = order.astype(F32)
        value = jnp.exp(0.5 * (logs + jnp.log(jnp.full((1, LANES), 0.5, F32)) + m * log_cos))
        return jnp.where(odd, sign * jnp.sqrt(2.0 * m + 3.0) * x * value, value)

    seed1 = seed(pair_lane, logs1)
    seed2 = jnp.where(odd & (pair_lane < 1), 0.0, -seed(M - 1 - pair_lane, logs2))
    zero = jnp.zeros((high, LANES), F32)
    group = 32

    def steps(base, n, carry):
        last, before = carry
        for i in range(n):
            a, b, g = (coef_ref[c, pl.ds(base + i, 1), :] for c in range(3))
            tail = jnp.where(first_lane == base + i, seed2, g * before)
            now = (a * x2 - b) * last - tail
            p_ref[base + i, pl.ds(0, high), :] = now
            last, before = now, last
        return last, before

    carry = lax.fori_loop(
        0, slots // group, lambda t, c: steps(pl.multiple_of(t * group, group), group, c), (zero, seed1)
    )
    rest = slots % group
    if rest:
        steps(slots - rest, rest, carry)
    stride = p_ref.shape[1]


def weights_rows(p_ref, pt_ref, high, slots):
    blocks = -(-slots // LANES)
    for h in range(high):
        for block in range(blocks):
            tile = p_ref[pl.ds(block * LANES, LANES), h, :]
            pt_ref[pl.ds(h * LANES, LANES), pl.ds(block * LANES, LANES)] = tile.T


def project(pair_ref, pt_ref, spec, s, i, stage_ref, loc_ref, rem_ref, sets, slots, high):
    low = LANES // (2 * sets)
    band = high * low
    acc = None
    pair = pair_ref[s]
    for q in range(2):
        row = (q * sets + s) * low
        w = jnp.concatenate([pt_ref[pl.ds(h * LANES + row, low), pl.ds(0, slots)] for h in range(high)], axis=0)
        slot = lax.broadcasted_iota(jnp.int32, (band, slots), 1)
        first = slot < (M - pair + 1 - q) // 2
        lhs = jnp.concatenate([jnp.where(first, w, 0.0), jnp.where(first, 0.0, w)], axis=0).astype(BF16)
        part = jnp.dot(lhs, spec[q], preferred_element_type=F32)
        acc = part if acc is None else acc + part
    cols = acc.shape[1] // LANES
    for j in range(2):
        for c in range(cols):
            stage_ref[pl.ds(c * 2 + j, band, stride=2 * cols), :] = acc[j * band : (j + 1) * band, c * LANES : (c + 1) * LANES]
    cut = loc_ref.shape[1]
    loc_ref[i] = stage_ref[pl.ds(0, cut), :].astype(BF16)
    rem_ref[i] = stage_ref[pl.ds(cut, rem_ref.shape[1]), :].astype(BF16)


def first_kernel(pair_ref, sign_ref, x_ref, spec_ref, loc_ref, rem_ref, pt_ref, tab_ref, coef_ref, p_ref, buf_ref, stage_ref, sems, *, sets, slots, n):
    high = x_ref.shape[0]
    copies = [pltpu.make_async_copy(spec_ref.at[i], buf_ref.at[i], sems.at[i]) for i in range(n)]
    for copy in copies:
        copy.start()
    legendre(pair_ref, sign_ref, x_ref, tab_ref, coef_ref, p_ref, pt_ref, sets, slots)
    weights_rows(p_ref, pt_ref, high, slots)
    for i in range(n):
        copies[i].wait()
        project(pair_ref, pt_ref, buf_ref.at[i], i, i, stage_ref, loc_ref, rem_ref, sets, slots, high)


def next_kernel(pair_ref, pt_ref, spec_ref, loc_ref, rem_ref, buf_ref, stage_ref, sems, *, sets, slots, n, begin, high):
    copies = [pltpu.make_async_copy(spec_ref.at[begin + i], buf_ref.at[i], sems.at[i]) for i in range(n)]
    for copy in copies:
        copy.start()
    for i in range(n):
        copies[i].wait()
        project(pair_ref, pt_ref, buf_ref.at[i], begin + i, i, stage_ref, loc_ref, rem_ref, sets, slots, high)


def place_kernel(base_ref, *refs, plan, alias):
    parts = refs[: len(plan)]
    out_ref, sems = refs[-2], refs[-1]
    copies = []
    for part, (which, begin) in zip(parts, plan):
        for i in range(part.shape[0]):
            copies.append(
                pltpu.make_async_copy(part.at[i], out_ref.at[:, base_ref[which] + begin + i], sems.at[len(copies)])
            )
    for copy in copies:
        copy.start()
    for copy in copies:
        copy.wait()


def place(bases, parts, plan, shape, out=None):
    count = sum(part.shape[0] for part in parts)
    extra = () if out is None else (out,)
    return pl.pallas_call(
        functools.partial(place_kernel, plan=plan, alias=out is not None),
        in_specs=[SMEM] + [ANY] * (len(parts) + len(extra)),
        out_specs=ANY,
        out_shape=jax.ShapeDtypeStruct(shape, BF16),
        scratch_shapes=[pltpu.SemaphoreType.DMA((count,))],
        input_output_aliases={} if out is None else {1 + len(parts): 0},
        compiler_params=PARAMS,
    )(bases, *parts, *extra)


def local(spectral, set_pair, lat_sines):
    sets, _, slots, cols = spectral.shape
    half = lax.axis_size("lat") // 2
    peers = lax.axis_size("ma")
    lat_index = lax.axis_index("lat")
    ma = lax.axis_index("ma")
    band = lat_sines.shape[0] // half
    own = band // peers
    low = LANES // (2 * sets)
    high = band // low
    cb = cols // LANES
    sign = jnp.where(lat_index < half, 1.0, -1.0).astype(F32).reshape(1)
    rows = (lat_index % half) * band + (ma * own + jnp.arange(band, dtype=jnp.int32)) % band
    x = jnp.tile(lat_sines[rows].reshape(high, low), (1, 2 * sets))
    padded = -(-slots // LANES) * LANES
    pt_shape = jax.ShapeDtypeStruct((high * LANES, padded), F32)

    def shapes(n):
        return [
            jax.ShapeDtypeStruct((n, own * 2 * cb, LANES), BF16),
            jax.ShapeDtypeStruct((n, (band - own) * 2 * cb, LANES), BF16),
        ]

    def scratch(n):
        return [
            pltpu.VMEM((n, 2, slots, cols), BF16),
            pltpu.VMEM((band * 2 * cb, LANES), F32),
            pltpu.SemaphoreType.DMA((n,)),
        ]

    begins = [sum(CHUNKS[:k]) for k in range(len(CHUNKS))]
    locs, sent = [], []
    for k, n in enumerate(CHUNKS):
        if k == 0:
            loc, rem, pt = pl.pallas_call(
                functools.partial(first_kernel, sets=sets, slots=slots, n=n),
                in_specs=[SMEM, SMEM, VMEM, ANY],
                out_specs=[VMEM] * 3,
                out_shape=shapes(n) + [pt_shape],
                scratch_shapes=[
                    pltpu.VMEM((6 * sets, padded), F32),
                    pltpu.VMEM((3, padded, LANES), F32),
                    pltpu.VMEM((padded, -(-high // 8) * 8, LANES), F32),
                ]
                + scratch(n),
                compiler_params=PARAMS,
            )(set_pair, sign, x, spectral)
        else:
            loc, rem = pl.pallas_call(
                functools.partial(next_kernel, sets=sets, slots=slots, n=n, begin=begins[k], high=high),
                in_specs=[SMEM, VMEM, ANY],
                out_specs=[VMEM] * 2,
                out_shape=shapes(n),
                scratch_shapes=scratch(n),
                compiler_params=PARAMS,
            )(set_pair, pt, spectral)
        locs.append(loc.reshape(n, own, cb, 2, LANES))
        parts = rem.reshape(n, peers - 1, own * 2 * cb, LANES)
        got = []
        for d in range(1, peers):
            moved = lax.ppermute(parts[:, d - 1], "ma", [(i, (i + d) % peers) for i in range(peers)])
            got.append(moved.reshape(n, own, cb, 2, LANES))
        sent.append(got)
    bases = ((ma - jnp.arange(peers, dtype=jnp.int32)) % peers) * sets
    shape = (own, peers * sets, cb, 2, LANES)
    early = [(loc, (0, b)) for loc, b in zip(locs, begins)]
    late = []
    for k, got in enumerate(sent):
        (late if k == len(sent) - 1 else early).extend((g, (d + 1, begins[k])) for d, g in enumerate(got))
    out = place(bases, [p for p, _ in early], [w for _, w in early], shape)
    out = place(bases, [p for p, _ in late], [w for _, w in late], shape, out)
    return out.transpose(0, 1, 3, 2, 4).reshape(own, peers * sets, 2, cols)


def solution(mesh):
    placed = (P("ma", None, None, None), P("ma"), P())
    return jax.shard_map(
        local,
        mesh=mesh,
        in_specs=placed,
        out_specs=P(("lat", "ma"), None, None, None),
        check_vma=False,
    )
```

time: 313 us -> 34.8 us (0.11)
  local copies, waits for them, and re-layouts: 142 us -> 2.47 us
  other arithmetic: 132 us -> 0.04 us
  blocking collectives: 27.5 us -> 0 us
  Pallas kernels: 0 us -> 19.7 us
  matrix products: 7.22 us -> 0 us
  waiting for transfers between devices: 0 us -> 7.03 us
  starting transfers between devices: 0 us -> 5.29 us
  loops' own time: 3.68 us -> 0 us
    while x1397 -> x0, other arithmetic: 123 us -> none
    gather x6 -> x1, local copies, waits for them, and re-layouts: 116 us -> 0.97 us  [local(): x = jnp.tile(lat_sines[rows].reshape(high, low), (1, 2 * sets))]
    all_to_all x1 -> x0, blocking collectives: 27.5 us -> none  [local(): lax.all_to_all(combined, 'ma', split_axis=0, concat_axis=1, tiled=True)]
    pallas_call x0 -> x6, Pallas kernels: none -> 19.7 us  [the longest x3 10.6 us: local(): pl.pallas_call(functools.partial(next_kernel, sets=sets, slots=slots, n=n...]
    dynamic_update_slice x11 -> x0, local copies, waits for them, and re-layouts: 8.07 us -> none  [legendre_runs(): _, blocks_out = lax.scan(advance, (zero_state, zero_state), block_tables)]
    dot_general x2 -> x0, matrix products: 7.22 us -> none  [project(): jnp.einsum('stje,sec->tsjc', weights, coeffs, preferred_element_type=jnp....]
    ppermute x0 -> x4, waiting for transfers between devices: none -> 7.03 us  [local(): lax.ppermute(parts[:, d - 1], 'ma', [(i, (i + d) % peers) for i in range(...]
    dynamic_slice x88 -> x0, local copies, waits for them, and re-layouts: 5.67 us -> none  [legendre_runs(): _, blocks_out = lax.scan(advance, (zero_state, zero_state), block_tables)]
  transfers between devices with their start and end apart: 0 -> 4, of which waited for: 0 -> 2; matrix products, arithmetic and copies ran while one was open for 0% -> 0% of each run, Pallas kernels for 0% -> 36%
where the time goes in v1:
time: 34.8 us; the launch traced here: 34.6 us
  Pallas kernels  19.7 us (57%)
  waiting for transfers between devices  7.03 us (20%)
  starting transfers between devices  5.29 us (15%)
  local copies, waits for them, and re-layouts  2.47 us (7%)
    pallas_call x3, Pallas kernels, local(): pl.pallas_call(functools.partial(next_kernel, sets=sets, slots=slots, n=n...  10.6 us
    ppermute x4, waiting for transfers between devices, local(): lax.ppermute(parts[:, d - 1], 'ma', [(i, (i + d) % peers) for i in range(...  7.03 us
    pallas_call x1, Pallas kernels, local(): pl.pallas_call(functools.partial(first_kernel, sets=sets, slots=slots, n=...  6.05 us
    ppermute x4, starting transfers between devices, local(): lax.ppermute(parts[:, d - 1], 'ma', [(i, (i + d) % peers) for i in range(...  5.29 us
    pallas_call x2, Pallas kernels, place(): pl.pallas_call(functools.partial(place_kernel, plan=plan, alias=out is no...  3.09 us
    unnamed x4, local copies, waits for them, and re-layouts  1.31 us
    gather x1, local copies, waits for them, and re-layouts, local(): x = jnp.tile(lat_sines[rows].reshape(high, low), (1, 2 * sets))  0.97 us
  transfers between devices with their start and end apart: 4, of which 2 were waited for; matrix products, arithmetic and copies ran while one was open for 0% of the time, Pallas kernels for 36%

profile of v1, /device:TPU:0, one launch (start us, length us, event | category | flops | bytes accessed | tf_op | source)
XLA Modules:
  0.0 34.6 jit_solution(15039389663524814556)
XLA Ops:
  0.0 0.0 copy-start
  0.0 0.7 %copy-done = f32[640]{0:T(1024)S(1)} copy-done((f32[640]{0:T(1024)S(1)}, f32[640]{0:T(1024)}, u32[]{:S(2)}) %copy-start) | copy-done | bytes 2584
  0.7 1.0 %gather_fusion = f32[80]{0:T(128)S(1)} fusion(f32[640]{0:T(1024)S(1)} %copy-done, s32[1024]{0:T(1024)S(1)} %pad_clamp_fusion), kind=kCustom, calls=%fused_computation | custom fusion | bytes 960 | tf_op jit(solution)/shard_map/gather | solution.py:220
  1.7 0.1 tile.10
  1.8 0.1 tile.12.x_ref
  1.9 0.0 copy-start.1
  1.9 0.6 %copy-done.1 = s32[8]{0:T(128)S(1)} copy-done((s32[8]{0:T(128)S(1)}, s32[8]{0:T(128)}, u32[]{:S(2)}) %copy-start.1) | copy-done | bytes 56
  2.5 6.1 %shard_map.37 = (bf16[2,480,128]{2,1,0:T(8,128)(2,1)S(1)}, bf16[2,480,128]{2,1,0:T(8,128)(2,1)S(1)}, f32[1280,768]{1,0:T(8,128)S(1)}) custom-call(s32[8]{0:T(128)S(1)} %copy-done.1, f32[1]{0:T(128)} %bitcast.sign_ref, f32[10,128]{1,0:T(8,128)S(1)} %tile.12.x_ref, bf16[8,2,648,768]{3,2,1,0:T(8,128)(2,1)} %spec_ref.7), custom_call_target="tpu_custom_call" | custom-call | tf_op jit(solution)/shard_map/pallas_call | solution.py:241
  8.6 3.0 %collective-permute-start.1 = (bf16[2,480,128]{2,1,0:T(8,128)(2,1)S(1)}, bf16[2,480,128]{2,1,0:T(8,128)(2,1)S(1)}, u32[]{:S(2)}, u32[]{:S(2)}) collective-permute-start(bf16[2,480,128]{2,1,0:T(8,128)(2,1)S(1)} %get-tuple-element.20), channel_id=1, source_target_pairs={{0,1},{1,0},{2,3},{3,2},{4,5},{5,4},{6,7},{7,6},{8,9},{9,8},{10,11... | collective-permute-start | bytes 737288 | tf_op jit(solution)/shard_map/ppermute | solution.py:267
  11.6 3.5 %shard_map.40 = (bf16[2,480,128]{2,1,0:T(8,128)(2,1)S(1)}, bf16[2,480,128]{2,1,0:T(8,128)(2,1)S(1)}) custom-call(s32[8]{0:T(128)S(1)} %copy-done.1, f32[1280,768]{1,0:T(8,128)S(1)} %get-tuple-element.14.pt_ref, bf16[8,2,648,768]{3,2,1,0:T(8,128)(2,1)} %spec_ref.7), custom_call_target="tpu_custom_call" | custom-call | tf_op jit(solution)/shard_map/pallas_call | solution.py:255
  15.2 0.1 collective-permute-start.3
  15.2 3.5 %shard_map.39 = (bf16[2,480,128]{2,1,0:T(8,128)(2,1)S(1)}, bf16[2,480,128]{2,1,0:T(8,128)(2,1)S(1)}) custom-call(s32[8]{0:T(128)S(1)} %copy-done.1, f32[1280,768]{1,0:T(8,128)S(1)} %get-tuple-element.14.pt_ref, bf16[8,2,648,768]{3,2,1,0:T(8,128)(2,1)} %spec_ref.7), custom_call_target="tpu_custom_call" | custom-call | tf_op jit(solution)/shard_map/pallas_call | solution.py:255
  18.8 2.1 %collective-permute-start.2 = (bf16[2,480,128]{2,1,0:T(8,128)(2,1)S(1)}, bf16[2,480,128]{2,1,0:T(8,128)(2,1)S(1)}, u32[]{:S(2)}, u32[]{:S(2)}) collective-permute-start(bf16[2,480,128]{2,1,0:T(8,128)(2,1)S(1)} %get-tuple-element.21), channel_id=1, source_target_pairs={{0,1},{1,0},{2,3},{3,2},{4,5},{5,4},{6,7},{7,6},{8,9},{9,8},{10,11... | collective-permute-start | bytes 737288 | tf_op jit(solution)/shard_map/ppermute | solution.py:267
  20.9 3.5 %shard_map.38 = (bf16[2,480,128]{2,1,0:T(8,128)(2,1)S(1)}, bf16[2,480,128]{2,1,0:T(8,128)(2,1)S(1)}) custom-call(s32[8]{0:T(128)S(1)} %copy-done.1, f32[1280,768]{1,0:T(8,128)S(1)} %get-tuple-element.14.pt_ref, bf16[8,2,648,768]{3,2,1,0:T(8,128)(2,1)} %spec_ref.7), custom_call_target="tpu_custom_call" | custom-call | tf_op jit(solution)/shard_map/pallas_call | solution.py:255
  24.4 0.1 collective-permute-start
  24.5 0.0 collective-permute-done.1
  24.5 0.0 collective-permute-done.3
  24.5 4.8 %collective-permute-done.2 = bf16[2,480,128]{2,1,0:T(8,128)(2,1)S(1)} collective-permute-done((bf16[2,480,128]{2,1,0:T(8,128)(2,1)S(1)}, bf16[2,480,128]{2,1,0:T(8,128)(2,1)S(1)}, u32[]{:S(2)}, u32[]{:S(2)}) %collective-permute-start.2) | collective-permute-done | bytes 245792 | tf_op jit(solution)/shard_map/ppermute | solution.py:267
  29.3 1.8 %shard_map.41.refs_1_ = bf16[40,16,6,2,128]{4,3,2,1,0:T(2,128)(2,1)} custom-call(s32[2]{0:T(128)S(1)} %fusion.base_ref, bf16[2,40,6,2,128]{4,3,2,1,0:T(2,128)(2,1)S(1)} %bitcast.14, bf16[2,40,6,2,128]{4,3,2,1,0:T(2,128)(2,1)S(1)} %bitcast.18, bf16[2,40,6,2,128]{4,3,2,1,0:T(2,128)(2,1)S(1)} %bitcast.16, bf16[2,40,6,2,128]{4,3,2,1,0:T(2,128)(2,1)S(1)} %bitcast.20, ...), custom_call_target="tpu_custom_call" | custom-call | tf_op jit(solution)/shard_map/pallas_call | solution.py:196
  31.2 2.2 %collective-permute-done = bf16[2,480,128]{2,1,0:T(8,128)(2,1)S(1)} collective-permute-done((bf16[2,480,128]{2,1,0:T(8,128)(2,1)S(1)}, bf16[2,480,128]{2,1,0:T(8,128)(2,1)S(1)}, u32[]{:S(2)}, u32[]{:S(2)}) %collective-permute-start) | collective-permute-done | bytes 245792 | tf_op jit(solution)/shard_map/ppermute | solution.py:267
  33.4 1.2 %shard_map.42 = bf16[40,16,6,2,128]{4,3,2,1,0:T(2,128)(2,1)} custom-call(s32[2]{0:T(128)S(1)} %fusion.base_ref, bf16[2,40,6,2,128]{4,3,2,1,0:T(2,128)(2,1)S(1)} %bitcast.21, bf16[40,16,6,2,128]{4,3,2,1,0:T(2,128)(2,1)} %shard_map.41.refs_1_), custom_call_target="tpu_custom_call", output_to_operand_aliasing={{}: (2, {})} | custom-call | tf_op jit(solution)/shard_map/pallas_call | solution.py:196
  (4 shorter events, 0.0 us)
Async XLA Ops:
  0.0 0.7 %copy-start = (f32[640]{0:T(1024)S(1)}, f32[640]{0:T(1024)}, u32[]{:S(2)}) copy-start(f32[640]{0:T(1024)} %param.5) | copy-start | bytes 7684
  1.9 0.7 %copy-start.1 = (s32[8]{0:T(128)S(1)}, s32[8]{0:T(128)}, u32[]{:S(2)}) copy-start(s32[8]{0:T(128)} %pair_ref.7) | copy-start | bytes 100
  8.6 15.9 %collective-permute-start.1 = (bf16[2,480,128]{2,1,0:T(8,128)(2,1)S(1)}, bf16[2,480,128]{2,1,0:T(8,128)(2,1)S(1)}, u32[]{:S(2)}, u32[]{:S(2)}) collective-permute-start(bf16[2,480,128]{2,1,0:T(8,128)(2,1)S(1)} %get-tuple-element.20), channel_id=1, source_target_pairs={{0,1},{1,0},{2,3},{3,2},{4,5},{5,4},{6,7},{7,6},{8,9},{9,8},{10,11... | collective-permute-start | bytes 737288 | tf_op jit(solution)/shard_map/ppermute | solution.py:267
  15.2 9.3 %collective-permute-start.3 = (bf16[2,480,128]{2,1,0:T(8,128)(2,1)S(1)}, bf16[2,480,128]{2,1,0:T(8,128)(2,1)S(1)}, u32[]{:S(2)}, u32[]{:S(2)}) collective-permute-start(bf16[2,480,128]{2,1,0:T(8,128)(2,1)S(1)} %get-tuple-element.22), channel_id=1, source_target_pairs={{0,1},{1,0},{2,3},{3,2},{4,5},{5,4},{6,7},{7,6},{8,9},{9,8},{10,11... | collective-permute-start | bytes 737288 | tf_op jit(solution)/shard_map/ppermute | solution.py:267
  18.8 10.5 %collective-permute-start.2 = (bf16[2,480,128]{2,1,0:T(8,128)(2,1)S(1)}, bf16[2,480,128]{2,1,0:T(8,128)(2,1)S(1)}, u32[]{:S(2)}, u32[]{:S(2)}) collective-permute-start(bf16[2,480,128]{2,1,0:T(8,128)(2,1)S(1)} %get-tuple-element.21), channel_id=1, source_target_pairs={{0,1},{1,0},{2,3},{3,2},{4,5},{5,4},{6,7},{7,6},{8,9},{9,8},{10,11... | collective-permute-start | bytes 737288 | tf_op jit(solution)/shard_map/ppermute | solution.py:267
  24.4 9.0 %collective-permute-start = (bf16[2,480,128]{2,1,0:T(8,128)(2,1)S(1)}, bf16[2,480,128]{2,1,0:T(8,128)(2,1)S(1)}, u32[]{:S(2)}, u32[]{:S(2)}) collective-permute-start(bf16[2,480,128]{2,1,0:T(8,128)(2,1)S(1)} %get-tuple-element.15), channel_id=1, source_target_pairs={{0,1},{1,0},{2,3},{3,2},{4,5},{5,4},{6,7},{7,6},{8,9},{9,8},{10,11... | collective-permute-start | bytes 737288 | tf_op jit(solution)/shard_map/ppermute | solution.py:267

commit v2 on v1

v2 whole, which is shorter than its diff:
```python
import functools

import jax
import jax.numpy as jnp
from jax import lax
from jax.experimental import pallas as pl
from jax.experimental.pallas import tpu as pltpu
from jax.sharding import PartitionSpec as P


M = 1280
LANES = 128
F32 = jnp.float32
BF16 = jnp.bfloat16
CHUNKS = (1, 2, 2, 2, 1)
PIECES = 4
VMEM = pl.BlockSpec(memory_space=pltpu.VMEM)
SMEM = pl.BlockSpec(memory_space=pltpu.SMEM)
ANY = pl.BlockSpec(memory_space=pl.ANY)
HBM = pl.BlockSpec(memory_space=pltpu.HBM)
PARAMS = pltpu.CompilerParams(vmem_limit_bytes=40 << 20)


class Layout:
    def __init__(self, sets, slots, cols, band, own):
        self.sets, self.slots, self.cols, self.band, self.own = sets, slots, cols, band, own
        self.rows = 2 * sets
        self.low = LANES // self.rows
        self.blocks = -(-slots // LANES)
        self.padded = self.blocks * LANES
        self.cb = cols // LANES
        self.split = own % self.low == 0
        self.per_row = 2 * self.cb

    def high(self, count):
        return count // self.low

    def pitch(self, count):
        return -(-self.high(count) // 8) * 8


def coefficients(slot, parity, pair, first_count, count):
    first = slot < first_count
    order = jnp.where(first, pair, M - 1 - pair)
    offset = jnp.where(first, 2 * slot, 2 * (slot - first_count)) + parity
    valid = (offset >= 2) & (slot < count)
    degree = (order + offset).astype(F32)
    square = order.astype(F32) * order.astype(F32)

    def parts(k):
        return k * k - square, 4.0 * k * k - 1.0

    (u0, d0), (u1, d1), (u2, d2), (u3, d3) = (parts(degree - back) for back in range(4))
    u0 = jnp.where(valid, u0, 1.0)
    u1 = jnp.where(valid, u1, 1.0)
    a = jnp.sqrt((d1 / u1) * (d0 / u0))
    b = u1 / d1 + u2 / d2
    g = a * jnp.sqrt(jnp.maximum((u2 / d2) * (u3 / d3), 0.0))
    a, ab, g = (jnp.where(valid, value, 0.0) for value in (a, a * b, g))
    return a, ab, jnp.where(slot == 0, -1.0, g)


def table_block(lay, pair_ref, tab_ref, coef_ref, block):
    rows, sets, low = lay.rows, lay.sets, lay.low
    sub = lax.broadcasted_iota(jnp.int32, (rows, 1), 0)
    pair = jnp.zeros((rows, 1), jnp.int32)
    for s in range(sets):
        pair = jnp.where(sub % sets == s, pair_ref[s], pair)
    parity = sub // sets
    first_count = (M - pair + 1 - parity) // 2
    count = first_count + (pair + 2 - parity) // 2
    here = pl.ds(block * LANES, LANES)
    slot = lax.broadcasted_iota(jnp.int32, (rows, LANES), 1) + block * LANES
    for c, table in enumerate(coefficients(slot, parity, pair, first_count, count)):
        tab_ref[pl.ds(c * rows, rows), here] = table
    for c in range(3):
        wide = [jnp.broadcast_to(tab_ref[pl.ds(c * rows + r, 1), here], (low, LANES)) for r in range(rows)]
        coef_ref[c, here, :] = jnp.concatenate(wide, axis=0).T


def lane_values(lay, pair_ref):
    qs = lax.broadcasted_iota(jnp.int32, (1, LANES), 1) // lay.low
    pair = jnp.zeros((1, LANES), jnp.int32)
    for s in range(lay.sets):
        pair = jnp.where(qs % lay.sets == s, pair_ref[s], pair)
    return pair, qs // lay.sets


def seeds(lay, pair_ref, sign, x):
    sets = lay.sets
    sub = lax.broadcasted_iota(jnp.int32, (sets, 1), 0)
    column = jnp.zeros((sets, 1), jnp.int32)
    for s in range(sets):
        column = jnp.where(sub == s, pair_ref[s], column)
    lane_set = (lax.broadcasted_iota(jnp.int32, (sets, LANES), 1) // lay.low) % sets
    own_set = lane_set == lax.broadcasted_iota(jnp.int32, (sets, LANES), 0)
    pair, parity = lane_values(lay, pair_ref)
    odd = parity > 0
    log_cos = jnp.log(1.0 - x * x)

    def start(order_column, order):
        product = jnp.ones((sets, LANES), F32)
        for block in range(M // LANES):
            k = lax.broadcasted_iota(jnp.int32, (sets, LANES), 1) + (block * LANES + 1)
            product = product * jnp.where(k <= order_column, 1.0 + 0.5 / k.astype(F32), 1.0)
        logs = jnp.sum(jnp.log(product), axis=1, keepdims=True)
        logs = jnp.sum(jnp.where(own_set, logs, 0.0), axis=0, keepdims=True)
        m = order.astype(F32)
        value = jnp.exp(0.5 * (logs + jnp.log(jnp.full((1, LANES), 0.5, F32)) + m * log_cos))
        return jnp.where(odd, sign * jnp.sqrt(2.0 * m + 3.0) * x * value, value)

    first = start(column, pair)
    second = start(M - 1 - column, M - 1 - pair)
    return first, jnp.where(odd & (pair < 1), 0.0, -second)


def gather_rows(lay, sines_ref, begin, first_row, count):
    high = lay.high(count)
    lo = lax.broadcasted_iota(jnp.int32, (high, LANES), 1) % lay.low
    hi = lax.broadcasted_iota(jnp.int32, (high, LANES), 0)
    x = jnp.zeros((high, LANES), F32)
    for h in range(high):
        line = jnp.zeros((1, LANES), F32)
        for l in range(lay.low):
            row = first_row + (h * lay.low + l)
            row = jnp.where(row >= lay.band, row - lay.band, row)
            line = jnp.where(lo[:1] == l, sines_ref[begin + row], line)
        x = jnp.where(hi == h, line, x)
    return x


def legendre(lay, pair_ref, sign, x, coef_ref, p_ref, pt_ref, count, table):
    high, pitch = lay.high(count), lay.pitch(count)
    seed1, seed2 = seeds(lay, pair_ref, sign, x)
    pair, parity = lane_values(lay, pair_ref)
    switch = (M - pair + 1 - parity) // 2
    x2 = x * x
    last, before = jnp.zeros((high, LANES), F32), seed1

    def turn(block, h):
        n = min(LANES, lay.slots - block * LANES)
        tile = p_ref[pl.ds(block * LANES * pitch + h, n, stride=pitch), :]
        pt_ref[pl.ds(h * LANES, LANES), pl.ds(block * LANES, n)] = tile.T

    for block in range(lay.blocks):
        n = min(LANES, lay.slots - block * LANES)
        for i in range(n):
            slot = block * LANES + i
            if i == LANES // 8 and block + 1 < lay.blocks and table is not None:
                table(block + 1)
            if block and i >= LANES // 4 and (i - LANES // 4) % 8 == 0 and (i - LANES // 4) // 8 < high and n == LANES:
                turn(block - 1, (i - LANES // 4) // 8)
            a, b, g = (coef_ref[c, pl.ds(slot, 1), :] for c in range(3))
            tail = jnp.where(switch == slot, seed2, g * before) if slot >= 2 else g * before
            now = (a * x2 - b) * last - tail
            p_ref[pl.ds(slot * pitch, high), :] = now
            last, before = now, last
    whole = lay.slots // LANES
    for block in range(whole - 1, lay.blocks):
        for h in range(high):
            turn(block, h)


def project(lay, pair_ref, pt_ref, spec, s, stage_ref, count):
    acc = None
    pair = pair_ref[s]
    for q in range(2):
        row = (q * lay.sets + s) * lay.low
        w = jnp.concatenate(
            [pt_ref[pl.ds(h * LANES + row, lay.low), pl.ds(0, lay.slots)] for h in range(lay.high(count))], axis=0
        )
        first = lax.broadcasted_iota(jnp.int32, (count, lay.slots), 1) < (M - pair + 1 - q) // 2
        lhs = jnp.concatenate([jnp.where(first, w, 0.0), jnp.where(first, 0.0, w)], axis=0).astype(BF16)
        part = jnp.dot(lhs, spec[q], preferred_element_type=F32)
        acc = part if acc is None else acc + part
    for j in range(2):
        for c in range(lay.cb):
            stage_ref[pl.ds(c * 2 + j, count, stride=lay.per_row), :] = acc[
                j * count : (j + 1) * count, c * LANES : (c + 1) * LANES
            ]


def fetches(lay, spec_ref, buf_ref, sems, begin, n):
    step = lay.slots // PIECES // 16 * 16
    edges = [step * k for k in range(PIECES)] + [lay.slots]
    return [
        [
            pltpu.make_async_copy(
                spec_ref.at[begin + i, q, pl.ds(edges[k], edges[k + 1] - edges[k])],
                buf_ref.at[i, q, pl.ds(edges[k], edges[k + 1] - edges[k])],
                sems.at[i, q, k],
            )
            for q in range(2)
            for k in range(PIECES)
        ]
        for i in range(n)
    ]


def project_sets(lay, pair_ref, pt_ref, copies, buf_ref, stage_ref, out_ref, begin, n, count):
    for i in range(n):
        for copy in copies[i]:
            copy.wait()
        project(lay, pair_ref, pt_ref, buf_ref.at[i], begin + i, stage_ref, count)
        out_ref[i] = stage_ref[...].astype(BF16)


def position():
    half = lax.axis_size("lat") // 2
    lat = lax.axis_index("lat")
    return jnp.where(lat < half, 1.0, -1.0).astype(F32), lat % half, lax.axis_index("ma")


def head_kernel(
    pair_hbm, sines_hbm, spec_ref, out_ref, pt_ref, coef_ref, pair_ref, sines_ref, tab_ref, p_ref, buf_ref, stage_ref, small, sems,
    *, lay, n, count, offset,
):
    copies = fetches(lay, spec_ref, buf_ref, sems, 0, n)
    pair_copy = pltpu.make_async_copy(pair_hbm, pair_ref, small.at[0])
    sines_copy = pltpu.make_async_copy(sines_hbm, sines_ref, small.at[1])
    pair_copy.start()
    sines_copy.start()
    for group in copies:
        for copy in group:
            copy.start()
    sign, band, ma = position()
    pair_copy.wait()
    table_block(lay, pair_ref, tab_ref, coef_ref, 0)
    sines_copy.wait()
    x = gather_rows(lay, sines_ref, band * lay.band, ma * lay.own + offset, count)
    legendre(
        lay, pair_ref, sign, x, coef_ref, p_ref, pt_ref, count,
        lambda block: table_block(lay, pair_ref, tab_ref, coef_ref, block),
    )
    project_sets(lay, pair_ref, pt_ref, copies, buf_ref, stage_ref, out_ref, 0, n, count)


def next_kernel(pair_ref, pt_ref, spec_ref, out_ref, buf_ref, stage_ref, sems, *, lay, n, begin, count):
    copies = fetches(lay, spec_ref, buf_ref, sems, begin, n)
    for group in copies:
        for copy in group:
            copy.start()
    project_sets(lay, pair_ref, pt_ref, copies, buf_ref, stage_ref, out_ref, begin, n, count)


def own_kernel(
    pair_ref, sines_ref, coef_ref, spec_ref, out_ref, pt_ref, p_ref, buf_ref, stage_ref, sems, *, lay, n, count
):
    copies = fetches(lay, spec_ref, buf_ref, sems, 0, n)
    for group in copies:
        for copy in group:
            copy.start()
    sign, band, ma = position()
    x = gather_rows(lay, sines_ref, band * lay.band, ma * lay.own, count)
    legendre(lay, pair_ref, sign, x, coef_ref, p_ref, pt_ref, count, None)
    project_sets(lay, pair_ref, pt_ref, copies, buf_ref, stage_ref, out_ref, 0, n, count)


def place_kernel(base_ref, *refs, plan):
    parts = refs[: len(plan)]
    out_ref, sems = refs[-2], refs[-1]
    copies = []
    for part, (which, begin) in zip(parts, plan):
        for i in range(part.shape[0]):
            target = out_ref.at[:, base_ref[which] + begin + i]
            copies.append(pltpu.make_async_copy(part.at[i], target, sems.at[len(copies)]))
    for copy in copies:
        copy.start()
    for copy in copies:
        copy.wait()


def place(bases, parts, plan, shape, out=None):
    count = sum(part.shape[0] for part in parts)
    extra = () if out is None else (out,)
    return pl.pallas_call(
        functools.partial(place_kernel, plan=plan),
        in_specs=[SMEM] + [ANY] * (len(parts) + len(extra)),
        out_specs=ANY,
        out_shape=jax.ShapeDtypeStruct(shape, BF16),
        scratch_shapes=[pltpu.SemaphoreType.DMA((count,))],
        input_output_aliases={} if out is None else {1 + len(parts): 0},
        compiler_params=PARAMS,
    )(bases, *parts, *extra)


def transform(spectral, set_pair, lat_sines):
    sets, _, slots, cols = spectral.shape
    half = lax.axis_size("lat") // 2
    peers = lax.axis_size("ma")
    ma = lax.axis_index("ma")
    band = lat_sines.shape[0] // half
    own = band // peers
    lay = Layout(sets, slots, cols, band, own)
    offset = own if lay.split else 0
    count = band - offset
    cb = lay.cb

    def values(rows):
        return [
            jax.ShapeDtypeStruct((lay.high(rows) * LANES, lay.padded), F32),
            pltpu.VMEM((lay.padded * lay.pitch(rows), LANES), F32),
        ]

    def sums(n, rows):
        return [
            jax.ShapeDtypeStruct((n, rows * lay.per_row, LANES), BF16),
            pltpu.VMEM((n, 2, slots, cols), BF16),
            pltpu.VMEM((rows * lay.per_row, LANES), F32),
            pltpu.SemaphoreType.DMA((n, 2, PIECES)),
        ]

    begins = [sum(CHUNKS[:k]) for k in range(len(CHUNKS))]
    made = []
    for k, n in enumerate(CHUNKS):
        shape, *scratch = sums(n, count)
        if k == 0:
            pt_shape, p_scratch = values(count)
            coef_shape = jax.ShapeDtypeStruct((3, lay.padded, LANES), F32)
            made_now, pt, coef = pl.pallas_call(
                functools.partial(head_kernel, lay=lay, n=n, count=count, offset=offset),
                in_specs=[HBM, HBM, HBM],
                out_specs=[VMEM] * 3,
                out_shape=[shape, pt_shape, coef_shape],
                scratch_shapes=[
                    pltpu.SMEM(set_pair.shape, jnp.int32),
                    pltpu.SMEM(lat_sines.shape, F32),
                    pltpu.VMEM((3 * lay.rows, lay.padded), F32),
                    p_scratch,
                    *scratch[:2],
                    pltpu.SemaphoreType.DMA((2,)),
                    scratch[2],
                ],
                compiler_params=PARAMS,
            )(*(pltpu.with_memory_space_constraint(v, pltpu.HBM) for v in (set_pair, lat_sines)), spectral)
        else:
            made_now = pl.pallas_call(
                functools.partial(next_kernel, lay=lay, n=n, begin=begins[k], count=count),
                in_specs=[SMEM, VMEM, HBM],
                out_specs=VMEM,
                out_shape=shape,
                scratch_shapes=scratch,
                compiler_params=PARAMS,
            )(set_pair, pt, spectral)
        made.append(made_now.reshape(n, count // own, own * lay.per_row, LANES))

    first_peer = 0 if lay.split else 1
    early, late = [], []
    for k, (n, parts) in enumerate(zip(CHUNKS, made)):
        if not lay.split:
            early.append((parts[:, 0].reshape(n, own, cb, 2, LANES), (0, begins[k])))
        for d in range(1, peers):
            moved = lax.ppermute(parts[:, first_peer + d - 1], "ma", [(i, (i + d) % peers) for i in range(peers)])
            (late if k == len(CHUNKS) - 1 else early).append((moved.reshape(n, own, cb, 2, LANES), (d, begins[k])))
    if lay.split:
        shape, *scratch = sums(sets, own)
        pt_shape, p_scratch = values(own)
        mine = pl.pallas_call(
            functools.partial(own_kernel, lay=lay, n=sets, count=own),
            in_specs=[SMEM, SMEM, VMEM, HBM],
            out_specs=VMEM,
            out_shape=shape,
            scratch_shapes=[pltpu.VMEM(pt_shape.shape, F32), p_scratch, *scratch],
            compiler_params=PARAMS,
        )(set_pair, lat_sines, coef, spectral)
        early.append((mine.reshape(sets, own, cb, 2, LANES), (0, 0)))
    bases = ((ma - jnp.arange(peers, dtype=jnp.int32)) % peers) * sets
    shape = (own, peers * sets, cb, 2, LANES)
    out = place(bases, [p for p, _ in early], [w for _, w in early], shape)
    out = place(bases, [p for p, _ in late], [w for _, w in late], shape, out)
    return out.transpose(0, 1, 3, 2, 4).reshape(own, peers * sets, 2, cols)


def solution(mesh):
    placed = (P("ma", None, None, None), P("ma"), P())
    return jax.shard_map(
        transform,
        mesh=mesh,
        in_specs=placed,
        out_specs=P(("lat", "ma"), None, None, None),
        check_vma=False,
    )
```

time: 34.8 us -> 34.7 us (level)
  Pallas kernels: 19.7 us -> 27 us
  waiting for transfers between devices: 7.03 us -> 0.01 us
  local copies, waits for them, and re-layouts: 2.47 us -> 0.01 us
  starting transfers between devices: 5.29 us -> 7.28 us
    pallas_call x6 -> x8, Pallas kernels: 19.7 us -> 27 us  [the longest x4 13 us: transform(): pl.pallas_call(functools.partial(next_kernel, lay=lay, n=n, begin=begins[...]
    ppermute x4 -> x5, waiting for transfers between devices: 7.03 us -> 0.01 us  [transform(): lax.ppermute(parts[:, first_peer + d - 1], 'ma', [(i, (i + d) % peers) fo...]
    ppermute x4 -> x5, starting transfers between devices: 5.29 us -> 7.28 us  [transform(): lax.ppermute(parts[:, first_peer + d - 1], 'ma', [(i, (i + d) % peers) fo...]
    unnamed x4, local copies, waits for them, and re-layouts: 1.31 us -> 0.01 us
    gather x1 -> x0, local copies, waits for them, and re-layouts: 0.97 us -> none  [local(): x = jnp.tile(lat_sines[rows].reshape(high, low), (1, 2 * sets))]
  transfers between devices with their start and end apart: 4 -> 5, of which waited for: 2 -> 0; matrix products, arithmetic and copies ran while one was open for 0% -> 0% of each run, Pallas kernels for 36% -> 55%
where the time goes in v2:
time: 34.7 us; the launch traced here: 34.5 us
  Pallas kernels  27 us (78%)
  starting transfers between devices  7.28 us (21%)
    pallas_call x4, Pallas kernels, transform(): pl.pallas_call(functools.partial(next_kernel, lay=lay, n=n, begin=begins[...  13 us
    pallas_call x1, Pallas kernels, transform(): pl.pallas_call(functools.partial(own_kernel, lay=lay, n=sets, count=own),...  7.49 us
    ppermute x5, starting transfers between devices, transform(): lax.ppermute(parts[:, first_peer + d - 1], 'ma', [(i, (i + d) % peers) fo...  7.28 us
    pallas_call x1, Pallas kernels, transform(): pl.pallas_call(functools.partial(head_kernel, lay=lay, n=n, count=count,...  3.42 us
    pallas_call x2, Pallas kernels, place(): pl.pallas_call(functools.partial(place_kernel, plan=plan), in_specs=[SMEM...  3.09 us
  transfers between devices with their start and end apart: 5, of which 0 were waited for; matrix products, arithmetic and copies ran while one was open for 0% of the time, Pallas kernels for 55%

profile of v2, /device:TPU:0, one launch (start us, length us, event | category | flops | bytes accessed | tf_op | source)
XLA Modules:
  0.0 34.5 jit_solution(8622455980413773900)
XLA Ops:
  0.0 0.0 copy-start
  0.0 3.4 %shard_map.37 = (bf16[1,480,128]{2,1,0:T(8,128)(2,1)S(1)}, f32[640,768]{1,0:T(8,128)S(1)}, f32[3,768,128]{2,1,0:T(8,128)S(1)}) custom-call(s32[8]{0:T(128)} %pair_ref.9, f32[640]{0:T(1024)} %sines_ref.1, bf16[8,2,648,768]{3,2,1,0:T(8,128)(2,1)} %spec_ref.11), custom_call_target="tpu_custom_call" | custom-call | tf_op jit(solution)/shard_map/pallas_call | solution.py:320
  3.4 0.0 copy-done
  3.4 3.4 %shard_map.39 = bf16[2,480,128]{2,1,0:T(8,128)(2,1)S(1)} custom-call(s32[8]{0:T(128)S(1)} %copy-done, f32[640,768]{1,0:T(8,128)S(1)} %get-tuple-element.8.pt_ref, bf16[8,2,648,768]{3,2,1,0:T(8,128)(2,1)} %spec_ref.11), custom_call_target="tpu_custom_call" | custom-call | tf_op jit(solution)/shard_map/pallas_call | solution.py:337
  6.9 3.0 %collective-permute-start.2 = (bf16[2,480,128]{2,1,0:T(8,128)(2,1)S(1)}, bf16[2,480,128]{2,1,0:T(8,128)(2,1)S(1)}, u32[]{:S(2)}, u32[]{:S(2)}) collective-permute-start(bf16[2,480,128]{2,1,0:T(8,128)(2,1)S(1)} %shard_map.39), channel_id=1, source_target_pairs={{0,1},{1,0},{2,3},{3,2},{4,5},{5,4},{6,7},{7,6},{8,9},{9,8},{10,11... | collective-permute-start | bytes 737288 | tf_op jit(solution)/shard_map/ppermute | solution.py:353
  9.9 3.4 %shard_map.40 = bf16[2,480,128]{2,1,0:T(8,128)(2,1)S(1)} custom-call(s32[8]{0:T(128)S(1)} %copy-done, f32[640,768]{1,0:T(8,128)S(1)} %get-tuple-element.8.pt_ref, bf16[8,2,648,768]{3,2,1,0:T(8,128)(2,1)} %spec_ref.11), custom_call_target="tpu_custom_call" | custom-call | tf_op jit(solution)/shard_map/pallas_call | solution.py:337
  13.4 0.1 collective-permute-start.3
  13.5 3.4 %shard_map.41 = bf16[2,480,128]{2,1,0:T(8,128)(2,1)S(1)} custom-call(s32[8]{0:T(128)S(1)} %copy-done, f32[640,768]{1,0:T(8,128)S(1)} %get-tuple-element.8.pt_ref, bf16[8,2,648,768]{3,2,1,0:T(8,128)(2,1)} %spec_ref.11), custom_call_target="tpu_custom_call" | custom-call | tf_op jit(solution)/shard_map/pallas_call | solution.py:337
  16.9 2.1 %collective-permute-start.4 = (bf16[2,480,128]{2,1,0:T(8,128)(2,1)S(1)}, bf16[2,480,128]{2,1,0:T(8,128)(2,1)S(1)}, u32[]{:S(2)}, u32[]{:S(2)}) collective-permute-start(bf16[2,480,128]{2,1,0:T(8,128)(2,1)S(1)} %shard_map.41), channel_id=1, source_target_pairs={{0,1},{1,0},{2,3},{3,2},{4,5},{5,4},{6,7},{7,6},{8,9},{9,8},{10,11... | collective-permute-start | bytes 737288 | tf_op jit(solution)/shard_map/ppermute | solution.py:353
  19.0 0.0 copy-start.1
  19.0 0.1 collective-permute-start.1
  19.1 2.7 %shard_map.38 = bf16[1,480,128]{2,1,0:T(8,128)(2,1)S(1)} custom-call(s32[8]{0:T(128)S(1)} %copy-done, f32[640,768]{1,0:T(8,128)S(1)} %get-tuple-element.8.pt_ref, bf16[8,2,648,768]{3,2,1,0:T(8,128)(2,1)} %spec_ref.11), custom_call_target="tpu_custom_call" | custom-call | tf_op jit(solution)/shard_map/pallas_call | solution.py:337
  21.8 2.0 %collective-permute-start = (bf16[1,480,128]{2,1,0:T(8,128)(2,1)S(1)}, bf16[1,480,128]{2,1,0:T(8,128)(2,1)S(1)}, u32[]{:S(2)}, u32[]{:S(2)}) collective-permute-start(bf16[1,480,128]{2,1,0:T(8,128)(2,1)S(1)} %shard_map.38), channel_id=1, source_target_pairs={{0,1},{1,0},{2,3},{3,2},{4,5},{5,4},{6,7},{7,6},{8,9},{9,8},{10,11... | collective-permute-start | bytes 368648 | tf_op jit(solution)/shard_map/ppermute | solution.py:353
  23.8 0.0 copy-done.1
  23.8 7.5 %shard_map.42 = bf16[8,480,128]{2,1,0:T(8,128)(2,1)S(1)} custom-call(s32[8]{0:T(128)S(1)} %copy-done, f32[640]{0:T(1024)S(1)} %copy-done.1, f32[3,768,128]{2,1,0:T(8,128)S(1)} %get-tuple-element.10.coef_ref, bf16[8,2,648,768]{3,2,1,0:T(8,128)(2,1)} %spec_ref.11), custom_call_target="tpu_custom_call" | custom-call | tf_op jit(solution)/shard_map/pallas_call | solution.py:358
  31.3 0.0 collective-permute-done.1
  31.3 0.0 collective-permute-done.2
  31.3 0.0 collective-permute-done.3
  31.3 0.0 collective-permute-done.4
  31.4 1.9 %shard_map.43.refs_1_ = bf16[40,16,6,2,128]{4,3,2,1,0:T(2,128)(2,1)} custom-call(s32[2]{0:T(128)S(1)} %fusion.base_ref, bf16[1,40,6,2,128]{4,3,2,1,0:T(2,128)(2,1)S(1)} %bitcast.14, bf16[2,40,6,2,128]{4,3,2,1,0:T(2,128)(2,1)S(1)} %bitcast.10, bf16[2,40,6,2,128]{4,3,2,1,0:T(2,128)(2,1)S(1)} %bitcast.11, bf16[2,40,6,2,128]{4,3,2,1,0:T(2,128)(2,1)S(1)} %bitcast.12, ...), custom_call_target="tpu_custom_call" | custom-call | tf_op jit(solution)/shard_map/pallas_call | solution.py:276
  33.3 0.0 collective-permute-done
  33.3 1.2 %shard_map.44 = bf16[40,16,6,2,128]{4,3,2,1,0:T(2,128)(2,1)} custom-call(s32[2]{0:T(128)S(1)} %fusion.base_ref, bf16[1,40,6,2,128]{4,3,2,1,0:T(2,128)(2,1)S(1)} %bitcast.13, bf16[40,16,6,2,128]{4,3,2,1,0:T(2,128)(2,1)} %shard_map.43.refs_1_), custom_call_target="tpu_custom_call", output_to_operand_aliasing={{}: (2, {})} | custom-call | tf_op jit(solution)/shard_map/pallas_call | solution.py:276
  (1 shorter events, 0.0 us)
Async XLA Ops:
  0.0 3.4 %copy-start = (s32[8]{0:T(128)S(1)}, s32[8]{0:T(128)}, u32[]{:S(2)}) copy-start(s32[8]{0:T(128)} %pair_ref.9) | copy-start | bytes 100
  6.9 24.4 %collective-permute-start.2 = (bf16[2,480,128]{2,1,0:T(8,128)(2,1)S(1)}, bf16[2,480,128]{2,1,0:T(8,128)(2,1)S(1)}, u32[]{:S(2)}, u32[]{:S(2)}) collective-permute-start(bf16[2,480,128]{2,1,0:T(8,128)(2,1)S(1)} %shard_map.39), channel_id=1, source_target_pairs={{0,1},{1,0},{2,3},{3,2},{4,5},{5,4},{6,7},{7,6},{8,9},{9,8},{10,11... | collective-permute-start | bytes 737288 | tf_op jit(solution)/shard_map/ppermute | solution.py:353
  13.4 18.0 %collective-permute-start.3 = (bf16[2,480,128]{2,1,0:T(8,128)(2,1)S(1)}, bf16[2,480,128]{2,1,0:T(8,128)(2,1)S(1)}, u32[]{:S(2)}, u32[]{:S(2)}) collective-permute-start(bf16[2,480,128]{2,1,0:T(8,128)(2,1)S(1)} %shard_map.40), channel_id=1, source_target_pairs={{0,1},{1,0},{2,3},{3,2},{4,5},{5,4},{6,7},{7,6},{8,9},{9,8},{10,11... | collective-permute-start | bytes 737288 | tf_op jit(solution)/shard_map/ppermute | solution.py:353
  16.9 14.4 %collective-permute-start.4 = (bf16[2,480,128]{2,1,0:T(8,128)(2,1)S(1)}, bf16[2,480,128]{2,1,0:T(8,128)(2,1)S(1)}, u32[]{:S(2)}, u32[]{:S(2)}) collective-permute-start(bf16[2,480,128]{2,1,0:T(8,128)(2,1)S(1)} %shard_map.41), channel_id=1, source_target_pairs={{0,1},{1,0},{2,3},{3,2},{4,5},{5,4},{6,7},{7,6},{8,9},{9,8},{10,11... | collective-permute-start | bytes 737288 | tf_op jit(solution)/shard_map/ppermute | solution.py:353
  19.0 4.8 %copy-start.1 = (f32[640]{0:T(1024)S(1)}, f32[640]{0:T(1024)}, u32[]{:S(2)}) copy-start(f32[640]{0:T(1024)} %sines_ref.1) | copy-start | bytes 7684
  19.0 12.3 %collective-permute-start.1 = (bf16[1,480,128]{2,1,0:T(8,128)(2,1)S(1)}, bf16[1,480,128]{2,1,0:T(8,128)(2,1)S(1)}, u32[]{:S(2)}, u32[]{:S(2)}) collective-permute-start(bf16[1,480,128]{2,1,0:T(8,128)(2,1)S(1)} %get-tuple-element.9), channel_id=1, source_target_pairs={{0,1},{1,0},{2,3},{3,2},{4,5},{5,4},{6,7},{7,6},{8,9},{9,8},{10,11... | collective-permute-start | bytes 368648 | tf_op jit(solution)/shard_map/ppermute | solution.py:353
  21.8 11.5 %collective-permute-start = (bf16[1,480,128]{2,1,0:T(8,128)(2,1)S(1)}, bf16[1,480,128]{2,1,0:T(8,128)(2,1)S(1)}, u32[]{:S(2)}, u32[]{:S(2)}) collective-permute-start(bf16[1,480,128]{2,1,0:T(8,128)(2,1)S(1)} %shard_map.38), channel_id=1, source_target_pairs={{0,1},{1,0},{2,3},{3,2},{4,5},{5,4},{6,7},{7,6},{8,9},{9,8},{10,11... | collective-permute-start | bytes 368648 | tf_op jit(solution)/shard_map/ppermute | solution.py:353

commit v3 on v2

--- a/solution.py
+++ b/solution.py
@@ -13,12 +13,13 @@
 F32 = jnp.float32
 BF16 = jnp.bfloat16
 CHUNKS = (1, 2, 2, 2, 1)
+AHEAD = 2
 PIECES = 4
 VMEM = pl.BlockSpec(memory_space=pltpu.VMEM)
 SMEM = pl.BlockSpec(memory_space=pltpu.SMEM)
 ANY = pl.BlockSpec(memory_space=pl.ANY)
 HBM = pl.BlockSpec(memory_space=pltpu.HBM)
-PARAMS = pltpu.CompilerParams(vmem_limit_bytes=40 << 20)
+PARAMS = pltpu.CompilerParams(vmem_limit_bytes=24 << 20)
 
 
 class Layout:
@@ -161,23 +162,30 @@
             turn(block, h)
 
 
-def project(lay, pair_ref, pt_ref, spec, s, stage_ref, count):
+def project(lay, pair_ref, groups, spec, s):
     acc = None
     pair = pair_ref[s]
+    here = pl.ds(0, lay.slots)
     for q in range(2):
-        row = (q * lay.sets + s) * lay.low
-        w = jnp.concatenate(
-            [pt_ref[pl.ds(h * LANES + row, lay.low), pl.ds(0, lay.slots)] for h in range(lay.high(count))], axis=0
-        )
-        first = lax.broadcasted_iota(jnp.int32, (count, lay.slots), 1) < (M - pair + 1 - q) // 2
-        lhs = jnp.concatenate([jnp.where(first, w, 0.0), jnp.where(first, 0.0, w)], axis=0).astype(BF16)
-        part = jnp.dot(lhs, spec[q], preferred_element_type=F32)
+        base = (q * lay.sets + s) * lay.low
+        parts = []
+        for pt_ref, count, _, _ in groups:
+            w = jnp.concatenate(
+                [pt_ref[pl.ds(h * LANES + base, lay.low), here] for h in range(lay.high(count))], axis=0
+            )
+            first = lax.broadcasted_iota(jnp.int32, (count, lay.slots), 1) < (M - pair + 1 - q) // 2
+            parts += [jnp.where(first, w, 0.0), jnp.where(first, 0.0, w)]
+        part = jnp.dot(jnp.concatenate(parts, axis=0).astype(BF16), spec[q], preferred_element_type=F32)
         acc = part if acc is None else acc + part
-    for j in range(2):
-        for c in range(lay.cb):
-            stage_ref[pl.ds(c * 2 + j, count, stride=lay.per_row), :] = acc[
-                j * count : (j + 1) * count, c * LANES : (c + 1) * LANES
-            ]
+    row = 0
+    for _, count, stage_ref, out_ref in groups:
+        for j in range(2):
+            for c in range(lay.cb):
+                stage_ref[pl.ds(c * 2 + j, count, stride=lay.per_row), :] = acc[
+                    row : row + count, c * LANES : (c + 1) * LANES
+                ]
+            row += count
+        out_ref[...] = stage_ref[...].astype(BF16)
 
 
 def fetches(lay, spec_ref, buf_ref, sems, begin, n):
@@ -197,12 +205,15 @@
     ]
 
 
-def project_sets(lay, pair_ref, pt_ref, copies, buf_ref, stage_ref, out_ref, begin, n, count):
-    for i in range(n):
-        for copy in copies[i]:
-            copy.wait()
-        project(lay, pair_ref, pt_ref, buf_ref.at[i], begin + i, stage_ref, count)
-        out_ref[i] = stage_ref[...].astype(BF16)
+def begin_all(copies):
+    for group in copies:
+        for copy in group:
+            copy.start()
+
+
+def wait_all(copies):
+    for copy in copies:
+        copy.wait()
 
 
 def position():
@@ -212,17 +223,16 @@
 
 
 def head_kernel(
-    pair_hbm, sines_hbm, spec_ref, out_ref, pt_ref, coef_ref, pair_ref, sines_ref, tab_ref, p_ref, buf_ref, stage_ref, small, sems,
+    pair_hbm, sines_hbm, spec_ref, out_ref, pt_ref, coef_ref, buf_ref, pair_ref, sines_ref, tab_ref, p_ref, stage_ref, small, sems,
     *, lay, n, count, offset,
 ):
-    copies = fetches(lay, spec_ref, buf_ref, sems, 0, n)
+    kept = buf_ref.shape[0]
+    copies = fetches(lay, spec_ref, buf_ref, sems, 0, kept)
     pair_copy = pltpu.make_async_copy(pair_hbm, pair_ref, small.at[0])
     sines_copy = pltpu.make_async_copy(sines_hbm, sines_ref, small.at[1])
     pair_copy.start()
     sines_copy.start()
-    for group in copies:
-        for copy in group:
-            copy.start()
+    begin_all(copies)
     sign, band, ma = position()
     pair_copy.wait()
     table_block(lay, pair_ref, tab_ref, coef_ref, 0)
@@ -232,28 +242,55 @@
         lay, pair_ref, sign, x, coef_ref, p_ref, pt_ref, count,
         lambda block: table_block(lay, pair_ref, tab_ref, coef_ref, block),
     )
-    project_sets(lay, pair_ref, pt_ref, copies, buf_ref, stage_ref, out_ref, 0, n, count)
-
-
-def next_kernel(pair_ref, pt_ref, spec_ref, out_ref, buf_ref, stage_ref, sems, *, lay, n, begin, count):
+    for i in range(kept):
+        wait_all(copies[i])
+        if i < n:
+            project(lay, pair_ref, [(pt_ref, count, stage_ref, out_ref.at[i])], buf_ref.at[i], i)
+
+
+def kept_kernel(pair_ref, pt_ref, buf_ref, out_ref, stage_ref, *, lay, begin, count):
+    for i in range(out_ref.shape[0]):
+        project(lay, pair_ref, [(pt_ref, count, stage_ref, out_ref.at[i])], buf_ref.at[begin + i], begin + i)
+
+
+def own_kernel(pair_ref, pt_ref, spec_ref, out_ref, buf_ref, stage_ref, sems, *, lay):
+    n = out_ref.shape[0]
+    copies = fetches(lay, spec_ref, buf_ref, sems, 0, n)
+    begin_all(copies)
+    for i in range(n):
+        wait_all(copies[i])
+        project(lay, pair_ref, [(pt_ref, lay.own, stage_ref, out_ref.at[i])], buf_ref.at[i], i)
+
+
+def late_kernel(*refs, lay, n, begin, count, make):
+    refs = list(refs)
+    pair_ref = refs.pop(0)
+    if make:
+        sines_ref, coef_ref = refs.pop(0), refs.pop(0)
+    pt_ref = refs.pop(0)
+    if lay.split and not make:
+        own_pt_ref = refs.pop(0)
+    spec_ref, out_ref = refs.pop(0), refs.pop(0)
+    if lay.split:
+        own_ref = refs.pop(0)
+    if make:
+        own_pt_ref = refs.pop(0)
+    buf_ref, stage_ref, sems = refs.pop(0), refs.pop(0), refs.pop(0)
     copies = fetches(lay, spec_ref, buf_ref, sems, begin, n)
-    for group in copies:
-        for copy in group:
-            copy.start()
-    project_sets(lay, pair_ref, pt_ref, copies, buf_ref, stage_ref, out_ref, begin, n, count)
-
-
-def own_kernel(
-    pair_ref, sines_ref, coef_ref, spec_ref, out_ref, pt_ref, p_ref, buf_ref, stage_ref, sems, *, lay, n, count
-):
-    copies = fetches(lay, spec_ref, buf_ref, sems, 0, n)
-    for group in copies:
-        for copy in group:
-            copy.start()
-    sign, band, ma = position()
-    x = gather_rows(lay, sines_ref, band * lay.band, ma * lay.own, count)
-    legendre(lay, pair_ref, sign, x, coef_ref, p_ref, pt_ref, count, None)
-    project_sets(lay, pair_ref, pt_ref, copies, buf_ref, stage_ref, out_ref, 0, n, count)
+    begin_all(copies)
+    if lay.split:
+        own_stage_ref = refs.pop(0)
+    if make:
+        p_ref = refs.pop(0)
+        sign, band, ma = position()
+        x = gather_rows(lay, sines_ref, band * lay.band, ma * lay.own, lay.own)
+        legendre(lay, pair_ref, sign, x, coef_ref, p_ref, own_pt_ref, lay.own, None)
+    for i in range(n):
+        wait_all(copies[i])
+        groups = [(pt_ref, count, stage_ref, out_ref.at[i])]
+        if lay.split:
+            groups.append((own_pt_ref, lay.own, own_stage_ref, own_ref.at[i]))
+        project(lay, pair_ref, groups, buf_ref.at[i], begin + i)
 
 
 def place_kernel(base_ref, *refs, plan):
@@ -296,74 +333,118 @@
     count = band - offset
     cb = lay.cb
 
-    def values(rows):
-        return [
-            jax.ShapeDtypeStruct((lay.high(rows) * LANES, lay.padded), F32),
-            pltpu.VMEM((lay.padded * lay.pitch(rows), LANES), F32),
-        ]
-
-    def sums(n, rows):
-        return [
-            jax.ShapeDtypeStruct((n, rows * lay.per_row, LANES), BF16),
-            pltpu.VMEM((n, 2, slots, cols), BF16),
-            pltpu.VMEM((rows * lay.per_row, LANES), F32),
-            pltpu.SemaphoreType.DMA((n, 2, PIECES)),
-        ]
+    split = lay.split
+    pt_shape = jax.ShapeDtypeStruct((lay.high(count) * LANES, lay.padded), F32)
+    own_pt_shape = jax.ShapeDtypeStruct((lay.high(own) * LANES, lay.padded), F32)
+    coef_shape = jax.ShapeDtypeStruct((3, lay.padded, LANES), F32)
+
+    def p_scratch(rows):
+        return pltpu.VMEM((lay.padded * lay.pitch(rows), LANES), F32)
+
+    def out_shape(n, rows):
+        return jax.ShapeDtypeStruct((n, rows * lay.per_row, LANES), BF16)
+
+    def stage(rows):
+        return pltpu.VMEM((rows * lay.per_row, LANES), F32)
+
+    def keep(value):
+        return pltpu.with_memory_space_constraint(value, pltpu.HBM)
+
+    def call(kernel, in_specs, shapes, scratch, args):
+        return pl.pallas_call(
+            kernel,
+            in_specs=in_specs,
+            out_specs=[VMEM] * len(shapes),
+            out_shape=shapes,
+            scratch_shapes=scratch,
+            compiler_params=PARAMS,
+        )(*args)
 
     begins = [sum(CHUNKS[:k]) for k in range(len(CHUNKS))]
-    made = []
+    kept = sum(CHUNKS[:AHEAD])
+    made, mine = [], []
     for k, n in enumerate(CHUNKS):
-        shape, *scratch = sums(n, count)
         if k == 0:
-            pt_shape, p_scratch = values(count)
-            coef_shape = jax.ShapeDtypeStruct((3, lay.padded, LANES), F32)
-            made_now, pt, coef = pl.pallas_call(
+            sent, pt, coef, buf = call(
                 functools.partial(head_kernel, lay=lay, n=n, count=count, offset=offset),
-                in_specs=[HBM, HBM, HBM],
-                out_specs=[VMEM] * 3,
-                out_shape=[shape, pt_shape, coef_shape],
-                scratch_shapes=[
+                [HBM] * 3,
+                [out_shape(n, count), pt_shape, coef_shape, jax.ShapeDtypeStruct((kept, 2, slots, cols), BF16)],
+                [
                     pltpu.SMEM(set_pair.shape, jnp.int32),
                     pltpu.SMEM(lat_sines.shape, F32),
                     pltpu.VMEM((3 * lay.rows, lay.padded), F32),
-                    p_scratch,
-                    *scratch[:2],
+                    p_scratch(count),
+                    stage(count),
                     pltpu.SemaphoreType.DMA((2,)),
-                    scratch[2],
+                    pltpu.SemaphoreType.DMA((kept, 2, PIECES)),
                 ],
-                compiler_params=PARAMS,
-            )(*(pltpu.with_memory_space_constraint(v, pltpu.HBM) for v in (set_pair, lat_sines)), spectral)
+                [keep(set_pair), keep(lat_sines), keep(spectral)],
+            )
+        elif k < AHEAD:
+            (sent,) = call(
+                functools.partial(kept_kernel, lay=lay, begin=begins[k], count=count),
+                [SMEM, VMEM, VMEM],
+                [out_shape(n, count)],
+                [stage(count)],
+                [set_pair, pt, buf],
+            )
         else:
-            made_now = pl.pallas_call(
-                functools.partial(next_kernel, lay=lay, n=n, begin=begins[k], count=count),
-                in_specs=[SMEM, VMEM, HBM],
-                out_specs=VMEM,
-                out_shape=shape,
-                scratch_shapes=scratch,
-                compiler_params=PARAMS,
-            )(set_pair, pt, spectral)
-        made.append(made_now.reshape(n, count // own, own * lay.per_row, LANES))
-
-    first_peer = 0 if lay.split else 1
+            make = split and k == AHEAD
+            operands = [(SMEM, set_pair)]
+            if make:
+                operands += [(SMEM, lat_sines), (VMEM, coef)]
+            operands.append((VMEM, pt))
+            if split and not make:
+                operands.append((VMEM, own_pt))
+            operands.append((HBM, keep(spectral)))
+            shapes = [out_shape(n, count)]
+            scratch = [
+                pltpu.VMEM((n, 2, slots, cols), BF16),
+                stage(count),
+                pltpu.SemaphoreType.DMA((n, 2, PIECES)),
+            ]
+            if split:
+                shapes.append(out_shape(n, own))
+                scratch.append(stage(own))
+            if make:
+                shapes.append(own_pt_shape)
+                scratch.append(p_scratch(own))
+            made_now = call(
+                functools.partial(late_kernel, lay=lay, n=n, begin=begins[k], count=count, make=make),
+                [spec for spec, _ in operands],
+                shapes,
+                scratch,
+                [value for _, value in operands],
+            )
+            sent = made_now[0]
+            if split:
+                mine.append((made_now[1], begins[k]))
+            if make:
+                own_pt = made_now[2]
+        made.append(sent.reshape(n, count // own, own * lay.per_row, LANES))
+
+    first_peer = 0 if split else 1
     early, late = [], []
     for k, (n, parts) in enumerate(zip(CHUNKS, made)):
-        if not lay.split:
-            early.append((parts[:, 0].reshape(n, own, cb, 2, LANES), (0, begins[k])))
+        if not split:
+            mine.append((parts[:, 0], begins[k]))
         for d in range(1, peers):
             moved = lax.ppermute(parts[:, first_peer + d - 1], "ma", [(i, (i + d) % peers) for i in range(peers)])
             (late if k == len(CHUNKS) - 1 else early).append((moved.reshape(n, own, cb, 2, LANES), (d, begins[k])))
-    if lay.split:
-        shape, *scratch = sums(sets, own)
-        pt_shape, p_scratch = values(own)
-        mine = pl.pallas_call(
-            functools.partial(own_kernel, lay=lay, n=sets, count=own),
-            in_specs=[SMEM, SMEM, VMEM, HBM],
-            out_specs=VMEM,
-            out_shape=shape,
-            scratch_shapes=[pltpu.VMEM(pt_shape.shape, F32), p_scratch, *scratch],
-            compiler_params=PARAMS,
-        )(set_pair, lat_sines, coef, spectral)
-        early.append((mine.reshape(sets, own, cb, 2, LANES), (0, 0)))
+    if split:
+        (first_own,) = call(
+            functools.partial(own_kernel, lay=lay),
+            [SMEM, VMEM, HBM],
+            [out_shape(kept, own)],
+            [
+                pltpu.VMEM((kept, 2, slots, cols), BF16),
+                stage(own),
+                pltpu.SemaphoreType.DMA((kept, 2, PIECES)),
+            ],
+            [set_pair, own_pt, keep(spectral)],
+        )
+        mine.append((first_own, 0))
+    early = [(part.reshape(part.shape[0], own, cb, 2, LANES), (0, begin)) for part, begin in mine] + early
     bases = ((ma - jnp.arange(peers, dtype=jnp.int32)) % peers) * sets
     shape = (own, peers * sets, cb, 2, LANES)
     out = place(bases, [p for p, _ in early], [w for _, w in early], shape)

time: 34.7 us -> 37.2 us (1.072)
  waiting for transfers between devices: 0.01 us -> 5.6 us
  Pallas kernels: 27 us -> 24.1 us
    ppermute x5, waiting for transfers between devices: 0.01 us -> 5.6 us  [transform(): lax.ppermute(parts[:, first_peer + d - 1], 'ma', [(i, (i + d) % peers) fo...]
    pallas_call x6, Pallas kernels: 24 us -> 21.1 us  [call(): pl.pallas_call(kernel, in_specs=in_specs, out_specs=[VMEM] * len(shapes),...]
  transfers between devices with their start and end apart: 5 -> 5, of which waited for: 0 -> 1; matrix products, arithmetic and copies ran while one was open for 0% -> 0% of each run, Pallas kernels for 55% -> 48%
where the time goes in v3:
time: 37.2 us; the launch traced here: 37.1 us
  Pallas kernels  24.1 us (65%)
  starting transfers between devices  7.22 us (19%)
  waiting for transfers between devices  5.6 us (15%)
    pallas_call x6, Pallas kernels, call(): pl.pallas_call(kernel, in_specs=in_specs, out_specs=[VMEM] * len(shapes),...  21.1 us
    ppermute x5, starting transfers between devices, transform(): lax.ppermute(parts[:, first_peer + d - 1], 'ma', [(i, (i + d) % peers) fo...  7.22 us
    ppermute x5, waiting for transfers between devices, transform(): lax.ppermute(parts[:, first_peer + d - 1], 'ma', [(i, (i + d) % peers) fo...  5.6 us
    pallas_call x2, Pallas kernels, place(): pl.pallas_call(functools.partial(place_kernel, plan=plan), in_specs=[SMEM...  3.09 us
  transfers between devices with their start and end apart: 5, of which 1 were waited for; matrix products, arithmetic and copies ran while one was open for 0% of the time, Pallas kernels for 48%

profile of v3, /device:TPU:0, one launch (start us, length us, event | category | flops | bytes accessed | tf_op | source)
XLA Modules:
  0.0 37.1 jit_solution(12487819231123458719)
XLA Ops:
  0.0 0.0 copy-start
  0.0 3.6 %shard_map.37 = (bf16[1,480,128]{2,1,0:T(8,128)(2,1)S(1)}, f32[640,768]{1,0:T(8,128)S(1)}, f32[3,768,128]{2,1,0:T(8,128)S(1)}, bf16[3,2,648,768]{3,2,1,0:T(8,128)(2,1)S(1)}) custom-call(s32[8]{0:T(128)} %pair_ref.3, f32[640]{0:T(1024)} %refs_1_.1, bf16[8,2,648,768]{3,2,1,0:T(8,128)(2,1)} %spec_ref.3), custom_call_target="tpu_custom_call" | custom-call | tf_op jit(solution)/shard_map/pallas_call | solution.py:354
  3.6 0.0 copy-done
  3.6 0.0 copy-start.1
  3.6 1.4 %shard_map.42 = bf16[2,480,128]{2,1,0:T(8,128)(2,1)S(1)} custom-call(s32[8]{0:T(128)S(1)} %copy-done, f32[640,768]{1,0:T(8,128)S(1)} %get-tuple-element.16.refs_3_.refs_1_.pt_ref, bf16[3,2,648,768]{3,2,1,0:T(8,128)(2,1)S(1)} %get-tuple-element.24.buf_ref), custom_call_target="tpu_custom_call" | custom-call | tf_op jit(solution)/shard_map/pallas_call | solution.py:354
  5.0 3.0 %collective-permute-start.2 = (bf16[2,480,128]{2,1,0:T(8,128)(2,1)S(1)}, bf16[2,480,128]{2,1,0:T(8,128)(2,1)S(1)}, u32[]{:S(2)}, u32[]{:S(2)}) collective-permute-start(bf16[2,480,128]{2,1,0:T(8,128)(2,1)S(1)} %shard_map.42), channel_id=1, source_target_pairs={{0,1},{1,0},{2,3},{3,2},{4,5},{5,4},{6,7},{7,6},{8,9},{9,8},{10,11... | collective-permute-start | bytes 737288 | tf_op jit(solution)/shard_map/ppermute | solution.py:432
  8.1 0.0 copy-done.1
  8.1 5.5 %shard_map.38 = (bf16[2,480,128]{2,1,0:T(8,128)(2,1)S(1)}, bf16[2,480,128]{2,1,0:T(8,128)(2,1)S(1)}, f32[640,768]{1,0:T(8,128)S(1)}) custom-call(s32[8]{0:T(128)S(1)} %copy-done, f32[640]{0:T(1024)S(1)} %copy-done.1, f32[3,768,128]{2,1,0:T(8,128)S(1)} %get-tuple-element.17.refs_2_, f32[640,768]{1,0:T(8,128)S(1)} %get-tuple-element.16.refs_3_.refs_1_.pt_ref, ...), custom_call_target="tpu_custom_call" | custom-call | tf_op jit(solution)/shard_map/pallas_call | solution.py:354
  13.5 3.7 %shard_map.40 = (bf16[2,480,128]{2,1,0:T(8,128)(2,1)S(1)}, bf16[2,480,128]{2,1,0:T(8,128)(2,1)S(1)}) custom-call(s32[8]{0:T(128)S(1)} %copy-done, f32[640,768]{1,0:T(8,128)S(1)} %get-tuple-element.16.refs_3_.refs_1_.pt_ref, f32[640,768]{1,0:T(8,128)S(1)} %get-tuple-element.18.refs_2_.pt_ref, bf16[8,2,648,768]{3,2,1,0:T(8,128)(2,1)} %spec_ref.3), custom_call_target="tpu_custom_call" | custom-call | tf_op jit(solution)/shard_map/pallas_call | solution.py:354
  17.3 0.1 collective-permute-start.4
  17.4 2.0 %collective-permute-start.3 = (bf16[2,480,128]{2,1,0:T(8,128)(2,1)S(1)}, bf16[2,480,128]{2,1,0:T(8,128)(2,1)S(1)}, u32[]{:S(2)}, u32[]{:S(2)}) collective-permute-start(bf16[2,480,128]{2,1,0:T(8,128)(2,1)S(1)} %get-tuple-element.25), channel_id=1, source_target_pairs={{0,1},{1,0},{2,3},{3,2},{4,5},{5,4},{6,7},{7,6},{8,9},{9,8},{10,11... | collective-permute-start | bytes 737288 | tf_op jit(solution)/shard_map/ppermute | solution.py:432
  19.4 0.1 collective-permute-start.1
  19.4 2.8 %shard_map.39 = (bf16[1,480,128]{2,1,0:T(8,128)(2,1)S(1)}, bf16[1,480,128]{2,1,0:T(8,128)(2,1)S(1)}) custom-call(s32[8]{0:T(128)S(1)} %copy-done, f32[640,768]{1,0:T(8,128)S(1)} %get-tuple-element.16.refs_3_.refs_1_.pt_ref, f32[640,768]{1,0:T(8,128)S(1)} %get-tuple-element.18.refs_2_.pt_ref, bf16[8,2,648,768]{3,2,1,0:T(8,128)(2,1)} %spec_ref.3), custom_call_target="tpu_custom_call" | custom-call | tf_op jit(solution)/shard_map/pallas_call | solution.py:354
  22.2 2.0 %collective-permute-start = (bf16[1,480,128]{2,1,0:T(8,128)(2,1)S(1)}, bf16[1,480,128]{2,1,0:T(8,128)(2,1)S(1)}, u32[]{:S(2)}, u32[]{:S(2)}) collective-permute-start(bf16[1,480,128]{2,1,0:T(8,128)(2,1)S(1)} %get-tuple-element.19), channel_id=1, source_target_pairs={{0,1},{1,0},{2,3},{3,2},{4,5},{5,4},{6,7},{7,6},{8,9},{9,8},{10,11... | collective-permute-start | bytes 368648 | tf_op jit(solution)/shard_map/ppermute | solution.py:432
  24.2 4.1 %shard_map.41 = bf16[3,480,128]{2,1,0:T(8,128)(2,1)S(1)} custom-call(s32[8]{0:T(128)S(1)} %copy-done, f32[640,768]{1,0:T(8,128)S(1)} %get-tuple-element.18.refs_2_.pt_ref, bf16[8,2,648,768]{3,2,1,0:T(8,128)(2,1)} %spec_ref.3), custom_call_target="tpu_custom_call" | custom-call | tf_op jit(solution)/shard_map/pallas_call | solution.py:354
  28.4 5.6 %collective-permute-done.1 = bf16[1,480,128]{2,1,0:T(8,128)(2,1)S(1)} collective-permute-done((bf16[1,480,128]{2,1,0:T(8,128)(2,1)S(1)}, bf16[1,480,128]{2,1,0:T(8,128)(2,1)S(1)}, u32[]{:S(2)}, u32[]{:S(2)}) %collective-permute-start.1) | collective-permute-done | bytes 122912 | tf_op jit(solution)/shard_map/ppermute | solution.py:432
  34.0 0.0 collective-permute-done.2
  34.0 0.0 collective-permute-done.4
  34.0 0.0 collective-permute-done.3
  34.0 1.9 %shard_map.43.refs_1_ = bf16[40,16,6,2,128]{4,3,2,1,0:T(2,128)(2,1)} custom-call(s32[2]{0:T(128)S(1)} %fusion.base_ref, bf16[2,40,6,2,128]{4,3,2,1,0:T(2,128)(2,1)S(1)} %bitcast.14, bf16[2,40,6,2,128]{4,3,2,1,0:T(2,128)(2,1)S(1)} %bitcast.15, bf16[1,40,6,2,128]{4,3,2,1,0:T(2,128)(2,1)S(1)} %bitcast.20, bf16[3,40,6,2,128]{4,3,2,1,0:T(2,128)(2,1)S(1)} %bitcast.12, ...), custom_call_target="tpu_custom_call" | custom-call | tf_op jit(solution)/shard_map/pallas_call | solution.py:313
  35.9 0.0 collective-permute-done
  35.9 1.2 %shard_map.44 = bf16[40,16,6,2,128]{4,3,2,1,0:T(2,128)(2,1)} custom-call(s32[2]{0:T(128)S(1)} %fusion.base_ref, bf16[1,40,6,2,128]{4,3,2,1,0:T(2,128)(2,1)S(1)} %bitcast.19, bf16[40,16,6,2,128]{4,3,2,1,0:T(2,128)(2,1)} %shard_map.43.refs_1_), custom_call_target="tpu_custom_call", output_to_operand_aliasing={{}: (2, {})} | custom-call | tf_op jit(solution)/shard_map/pallas_call | solution.py:313
  (1 shorter events, 0.0 us)
Async XLA Ops:
  0.0 3.6 %copy-start = (s32[8]{0:T(128)S(1)}, s32[8]{0:T(128)}, u32[]{:S(2)}) copy-start(s32[8]{0:T(128)} %pair_ref.3) | copy-start | bytes 100
  3.6 4.4 %copy-start.1 = (f32[640]{0:T(1024)S(1)}, f32[640]{0:T(1024)}, u32[]{:S(2)}) copy-start(f32[640]{0:T(1024)} %refs_1_.1) | copy-start | bytes 7684
  5.0 28.9 %collective-permute-start.2 = (bf16[2,480,128]{2,1,0:T(8,128)(2,1)S(1)}, bf16[2,480,128]{2,1,0:T(8,128)(2,1)S(1)}, u32[]{:S(2)}, u32[]{:S(2)}) collective-permute-start(bf16[2,480,128]{2,1,0:T(8,128)(2,1)S(1)} %shard_map.42), channel_id=1, source_target_pairs={{0,1},{1,0},{2,3},{3,2},{4,5},{5,4},{6,7},{7,6},{8,9},{9,8},{10,11... | collective-permute-start | bytes 737288 | tf_op jit(solution)/shard_map/ppermute | solution.py:432
  17.3 16.7 %collective-permute-start.4 = (bf16[2,480,128]{2,1,0:T(8,128)(2,1)S(1)}, bf16[2,480,128]{2,1,0:T(8,128)(2,1)S(1)}, u32[]{:S(2)}, u32[]{:S(2)}) collective-permute-start(bf16[2,480,128]{2,1,0:T(8,128)(2,1)S(1)} %get-tuple-element.26), channel_id=1, source_target_pairs={{0,1},{1,0},{2,3},{3,2},{4,5},{5,4},{6,7},{7,6},{8,9},{9,8},{10,11... | collective-permute-start | bytes 737288 | tf_op jit(solution)/shard_map/ppermute | solution.py:432
  17.4 16.6 %collective-permute-start.3 = (bf16[2,480,128]{2,1,0:T(8,128)(2,1)S(1)}, bf16[2,480,128]{2,1,0:T(8,128)(2,1)S(1)}, u32[]{:S(2)}, u32[]{:S(2)}) collective-permute-start(bf16[2,480,128]{2,1,0:T(8,128)(2,1)S(1)} %get-tuple-element.25), channel_id=1, source_target_pairs={{0,1},{1,0},{2,3},{3,2},{4,5},{5,4},{6,7},{7,6},{8,9},{9,8},{10,11... | collective-permute-start | bytes 737288 | tf_op jit(solution)/shard_map/ppermute | solution.py:432
  19.4 14.6 %collective-permute-start.1 = (bf16[1,480,128]{2,1,0:T(8,128)(2,1)S(1)}, bf16[1,480,128]{2,1,0:T(8,128)(2,1)S(1)}, u32[]{:S(2)}, u32[]{:S(2)}) collective-permute-start(bf16[1,480,128]{2,1,0:T(8,128)(2,1)S(1)} %get-tuple-element.23), channel_id=1, source_target_pairs={{0,1},{1,0},{2,3},{3,2},{4,5},{5,4},{6,7},{7,6},{8,9},{9,8},{10,11... | collective-permute-start | bytes 368648 | tf_op jit(solution)/shard_map/ppermute | solution.py:432
  22.2 13.6 %collective-permute-start = (bf16[1,480,128]{2,1,0:T(8,128)(2,1)S(1)}, bf16[1,480,128]{2,1,0:T(8,128)(2,1)S(1)}, u32[]{:S(2)}, u32[]{:S(2)}) collective-permute-start(bf16[1,480,128]{2,1,0:T(8,128)(2,1)S(1)} %get-tuple-element.19), channel_id=1, source_target_pairs={{0,1},{1,0},{2,3},{3,2},{4,5},{5,4},{6,7},{7,6},{8,9},{9,8},{10,11... | collective-permute-start | bytes 368648 | tf_op jit(solution)/shard_map/ppermute | solution.py:432

commit v4 on v3

--- a/solution.py
+++ b/solution.py
@@ -19,7 +19,7 @@
 SMEM = pl.BlockSpec(memory_space=pltpu.SMEM)
 ANY = pl.BlockSpec(memory_space=pl.ANY)
 HBM = pl.BlockSpec(memory_space=pltpu.HBM)
-PARAMS = pltpu.CompilerParams(vmem_limit_bytes=24 << 20)
+PARAMS = pltpu.CompilerParams(vmem_limit_bytes=16 << 20)
 
 
 class Layout:
@@ -251,15 +251,6 @@
 def kept_kernel(pair_ref, pt_ref, buf_ref, out_ref, stage_ref, *, lay, begin, count):
     for i in range(out_ref.shape[0]):
         project(lay, pair_ref, [(pt_ref, count, stage_ref, out_ref.at[i])], buf_ref.at[begin + i], begin + i)
-
-
-def own_kernel(pair_ref, pt_ref, spec_ref, out_ref, buf_ref, stage_ref, sems, *, lay):
-    n = out_ref.shape[0]
-    copies = fetches(lay, spec_ref, buf_ref, sems, 0, n)
-    begin_all(copies)
-    for i in range(n):
-        wait_all(copies[i])
-        project(lay, pair_ref, [(pt_ref, lay.own, stage_ref, out_ref.at[i])], buf_ref.at[i], i)
 
 
 def late_kernel(*refs, lay, n, begin, count, make):
@@ -293,39 +284,39 @@
         project(lay, pair_ref, groups, buf_ref.at[i], begin + i)
 
 
-def place_kernel(base_ref, *refs, plan):
+def place_kernel(*refs, plan, sets, peers):
     parts = refs[: len(plan)]
     out_ref, sems = refs[-2], refs[-1]
+    ma = lax.axis_index("ma")
     copies = []
-    for part, (which, begin) in zip(parts, plan):
+    for part, (back, begin) in zip(parts, plan):
+        base = lax.rem(ma + (peers - back), peers) * sets + begin
         for i in range(part.shape[0]):
-            target = out_ref.at[:, base_ref[which] + begin + i]
-            copies.append(pltpu.make_async_copy(part.at[i], target, sems.at[len(copies)]))
+            copies.append(pltpu.make_async_copy(part.at[i], out_ref.at[:, base + i], sems.at[len(copies)]))
     for copy in copies:
         copy.start()
     for copy in copies:
         copy.wait()
 
 
-def place(bases, parts, plan, shape, out=None):
+def place(parts, plan, shape, sets, peers, out=None):
     count = sum(part.shape[0] for part in parts)
     extra = () if out is None else (out,)
     return pl.pallas_call(
-        functools.partial(place_kernel, plan=plan),
-        in_specs=[SMEM] + [ANY] * (len(parts) + len(extra)),
+        functools.partial(place_kernel, plan=plan, sets=sets, peers=peers),
+        in_specs=[VMEM] * len(parts) + [ANY] * len(extra),
         out_specs=ANY,
         out_shape=jax.ShapeDtypeStruct(shape, BF16),
         scratch_shapes=[pltpu.SemaphoreType.DMA((count,))],
-        input_output_aliases={} if out is None else {1 + len(parts): 0},
+        input_output_aliases={} if out is None else {len(parts): 0},
         compiler_params=PARAMS,
-    )(bases, *parts, *extra)
+    )(*parts, *extra)
 
 
 def transform(spectral, set_pair, lat_sines):
     sets, _, slots, cols = spectral.shape
     half = lax.axis_size("lat") // 2
     peers = lax.axis_size("ma")
-    ma = lax.axis_index("ma")
     band = lat_sines.shape[0] // half
     own = band // peers
     lay = Layout(sets, slots, cols, band, own)
@@ -433,22 +424,17 @@
             (late if k == len(CHUNKS) - 1 else early).append((moved.reshape(n, own, cb, 2, LANES), (d, begins[k])))
     if split:
         (first_own,) = call(
-            functools.partial(own_kernel, lay=lay),
-            [SMEM, VMEM, HBM],
+            functools.partial(kept_kernel, lay=lay, begin=0, count=own),
+            [SMEM, VMEM, VMEM],
             [out_shape(kept, own)],
-            [
-                pltpu.VMEM((kept, 2, slots, cols), BF16),
-                stage(own),
-                pltpu.SemaphoreType.DMA((kept, 2, PIECES)),
-            ],
-            [set_pair, own_pt, keep(spectral)],
+            [stage(own)],
+            [set_pair, own_pt, buf],
         )
         mine.append((first_own, 0))
     early = [(part.reshape(part.shape[0], own, cb, 2, LANES), (0, begin)) for part, begin in mine] + early
-    bases = ((ma - jnp.arange(peers, dtype=jnp.int32)) % peers) * sets
     shape = (own, peers * sets, cb, 2, LANES)
-    out = place(bases, [p for p, _ in early], [w for _, w in early], shape)
-    out = place(bases, [p for p, _ in late], [w for _, w in late], shape, out)
+    out = place([p for p, _ in early], [w for _, w in early], shape, sets, peers)
+    out = place([p for p, _ in late], [w for _, w in late], shape, sets, peers, out)
     return out.transpose(0, 1, 3, 2, 4).reshape(own, peers * sets, 2, cols)
 
 

time: 37.2 us -> 38.4 us (1.032)
  waiting for transfers between devices: 5.6 us -> 10.2 us
  Pallas kernels: 24.1 us -> 20.8 us
    ppermute x5, waiting for transfers between devices: 5.6 us -> 10.2 us  [transform(): lax.ppermute(parts[:, first_peer + d - 1], 'ma', [(i, (i + d) % peers) fo...]
    pallas_call x6, Pallas kernels: 21.1 us -> 18.7 us  [call(): pl.pallas_call(kernel, in_specs=in_specs, out_specs=[VMEM] * len(shapes),...]
    pallas_call x2, Pallas kernels: 3.09 us -> 2.01 us  [place(): pl.pallas_call(functools.partial(place_kernel, plan=plan, sets=sets, peer...]
  transfers between devices with their start and end apart: 5 -> 5, of which waited for: 1 -> 2; matrix products, arithmetic and copies ran while one was open for 0% -> 0% of each run, Pallas kernels for 48% -> 19%
where the time goes in v4:
time: 38.4 us; the launch traced here: 38.3 us
  Pallas kernels  20.8 us (54%)
  waiting for transfers between devices  10.2 us (27%)
  starting transfers between devices  7.22 us (19%)
    pallas_call x6, Pallas kernels, call(): pl.pallas_call(kernel, in_specs=in_specs, out_specs=[VMEM] * len(shapes),...  18.7 us
    ppermute x5, waiting for transfers between devices, transform(): lax.ppermute(parts[:, first_peer + d - 1], 'ma', [(i, (i + d) % peers) fo...  10.2 us
    ppermute x5, starting transfers between devices, transform(): lax.ppermute(parts[:, first_peer + d - 1], 'ma', [(i, (i + d) % peers) fo...  7.22 us
    pallas_call x2, Pallas kernels, place(): pl.pallas_call(functools.partial(place_kernel, plan=plan, sets=sets, peer...  2.01 us
  transfers between devices with their start and end apart: 5, of which 2 were waited for; matrix products, arithmetic and copies ran while one was open for 0% of the time, Pallas kernels for 19%

profile of v4, /device:TPU:0, one launch (start us, length us, event | category | flops | bytes accessed | tf_op | source)
XLA Modules:
  0.0 38.3 jit_solution(12722332239782644560)
XLA Ops:
  0.0 0.0 copy-start
  0.0 0.0 copy-start.1
  0.0 3.6 %shard_map.37 = (bf16[1,480,128]{2,1,0:T(8,128)(2,1)S(1)}, f32[640,768]{1,0:T(8,128)S(1)}, f32[3,768,128]{2,1,0:T(8,128)S(1)}, bf16[3,2,648,768]{3,2,1,0:T(8,128)(2,1)S(1)}) custom-call(s32[8]{0:T(128)} %pair_ref.3, f32[640]{0:T(1024)} %refs_1_.1, bf16[8,2,648,768]{3,2,1,0:T(8,128)(2,1)} %refs_3_.3), custom_call_target="tpu_custom_call" | custom-call | tf_op jit(solution)/shard_map/pallas_call | solution.py:345
  3.6 0.0 copy-done
  3.6 0.0 copy-done.1
  3.6 5.5 %shard_map.38 = (bf16[2,480,128]{2,1,0:T(8,128)(2,1)S(1)}, bf16[2,480,128]{2,1,0:T(8,128)(2,1)S(1)}, f32[640,768]{1,0:T(8,128)S(1)}) custom-call(s32[8]{0:T(128)S(1)} %copy-done, f32[640]{0:T(1024)S(1)} %copy-done.1, f32[3,768,128]{2,1,0:T(8,128)S(1)} %get-tuple-element.17.refs_2_, f32[640,768]{1,0:T(8,128)S(1)} %get-tuple-element.16.refs_3_.refs_1_.pt_ref, ...), custom_call_target="tpu_custom_call" | custom-call | tf_op jit(solution)/shard_map/pallas_call | solution.py:345
  9.1 3.7 %shard_map.40 = (bf16[2,480,128]{2,1,0:T(8,128)(2,1)S(1)}, bf16[2,480,128]{2,1,0:T(8,128)(2,1)S(1)}) custom-call(s32[8]{0:T(128)S(1)} %copy-done, f32[640,768]{1,0:T(8,128)S(1)} %get-tuple-element.16.refs_3_.refs_1_.pt_ref, f32[640,768]{1,0:T(8,128)S(1)} %get-tuple-element.18.refs_2_.pt_ref, bf16[8,2,648,768]{3,2,1,0:T(8,128)(2,1)} %refs_3_.3), custom_call_target="tpu_custom_call" | custom-call | tf_op jit(solution)/shard_map/pallas_call | solution.py:345
  12.8 3.0 %collective-permute-start.4 = (bf16[2,480,128]{2,1,0:T(8,128)(2,1)S(1)}, bf16[2,480,128]{2,1,0:T(8,128)(2,1)S(1)}, u32[]{:S(2)}, u32[]{:S(2)}) collective-permute-start(bf16[2,480,128]{2,1,0:T(8,128)(2,1)S(1)} %get-tuple-element.26), channel_id=1, source_target_pairs={{0,1},{1,0},{2,3},{3,2},{4,5},{5,4},{6,7},{7,6},{8,9},{9,8},{10,11... | collective-permute-start | bytes 737288 | tf_op jit(solution)/shard_map/ppermute | solution.py:423
  15.9 0.1 collective-permute-start.3
  16.0 1.4 %shard_map.42 = bf16[2,480,128]{2,1,0:T(8,128)(2,1)S(1)} custom-call(s32[8]{0:T(128)S(1)} %copy-done, f32[640,768]{1,0:T(8,128)S(1)} %get-tuple-element.16.refs_3_.refs_1_.pt_ref, bf16[3,2,648,768]{3,2,1,0:T(8,128)(2,1)S(1)} %get-tuple-element.23.buf_ref), custom_call_target="tpu_custom_call" | custom-call | tf_op jit(solution)/shard_map/pallas_call | solution.py:345
  17.4 2.0 %collective-permute-start.2 = (bf16[2,480,128]{2,1,0:T(8,128)(2,1)S(1)}, bf16[2,480,128]{2,1,0:T(8,128)(2,1)S(1)}, u32[]{:S(2)}, u32[]{:S(2)}) collective-permute-start(bf16[2,480,128]{2,1,0:T(8,128)(2,1)S(1)} %shard_map.42), channel_id=1, source_target_pairs={{0,1},{1,0},{2,3},{3,2},{4,5},{5,4},{6,7},{7,6},{8,9},{9,8},{10,11... | collective-permute-start | bytes 737288 | tf_op jit(solution)/shard_map/ppermute | solution.py:423
  19.4 0.1 collective-permute-start.1
  19.4 2.8 %shard_map.39 = (bf16[1,480,128]{2,1,0:T(8,128)(2,1)S(1)}, bf16[1,480,128]{2,1,0:T(8,128)(2,1)S(1)}) custom-call(s32[8]{0:T(128)S(1)} %copy-done, f32[640,768]{1,0:T(8,128)S(1)} %get-tuple-element.16.refs_3_.refs_1_.pt_ref, f32[640,768]{1,0:T(8,128)S(1)} %get-tuple-element.18.refs_2_.pt_ref, bf16[8,2,648,768]{3,2,1,0:T(8,128)(2,1)} %refs_3_.3), custom_call_target="tpu_custom_call" | custom-call | tf_op jit(solution)/shard_map/pallas_call | solution.py:345
  22.2 2.0 %collective-permute-start = (bf16[1,480,128]{2,1,0:T(8,128)(2,1)S(1)}, bf16[1,480,128]{2,1,0:T(8,128)(2,1)S(1)}, u32[]{:S(2)}, u32[]{:S(2)}) collective-permute-start(bf16[1,480,128]{2,1,0:T(8,128)(2,1)S(1)} %get-tuple-element.19), channel_id=1, source_target_pairs={{0,1},{1,0},{2,3},{3,2},{4,5},{5,4},{6,7},{7,6},{8,9},{9,8},{10,11... | collective-permute-start | bytes 368648 | tf_op jit(solution)/shard_map/ppermute | solution.py:423
  24.2 1.8 %shard_map.41 = bf16[3,480,128]{2,1,0:T(8,128)(2,1)S(1)} custom-call(s32[8]{0:T(128)S(1)} %copy-done, f32[640,768]{1,0:T(8,128)S(1)} %get-tuple-element.18.refs_2_.pt_ref, bf16[3,2,648,768]{3,2,1,0:T(8,128)(2,1)S(1)} %get-tuple-element.23.buf_ref), custom_call_target="tpu_custom_call" | custom-call | tf_op jit(solution)/shard_map/pallas_call | solution.py:345
  26.0 9.8 %collective-permute-done.1 = bf16[1,480,128]{2,1,0:T(8,128)(2,1)S(1)} collective-permute-done((bf16[1,480,128]{2,1,0:T(8,128)(2,1)S(1)}, bf16[1,480,128]{2,1,0:T(8,128)(2,1)S(1)}, u32[]{:S(2)}, u32[]{:S(2)}) %collective-permute-start.1) | collective-permute-done | bytes 122912 | tf_op jit(solution)/shard_map/ppermute | solution.py:423
  35.9 0.0 collective-permute-done.4
  35.9 0.0 collective-permute-done.3
  35.9 0.0 collective-permute-done.2
  35.9 1.4 %shard_map.43.refs_1_ = bf16[40,16,6,2,128]{4,3,2,1,0:T(2,128)(2,1)} custom-call(bf16[2,40,6,2,128]{4,3,2,1,0:T(2,128)(2,1)S(1)} %bitcast.13, bf16[2,40,6,2,128]{4,3,2,1,0:T(2,128)(2,1)S(1)} %bitcast.14, bf16[1,40,6,2,128]{4,3,2,1,0:T(2,128)(2,1)S(1)} %bitcast.20, bf16[3,40,6,2,128]{4,3,2,1,0:T(2,128)(2,1)S(1)} %bitcast.12, ...), custom_call_target="tpu_custom_call" | custom-call | tf_op jit(solution)/shard_map/pallas_call | solution.py:305
  37.2 0.4 %collective-permute-done = bf16[1,480,128]{2,1,0:T(8,128)(2,1)S(1)} collective-permute-done((bf16[1,480,128]{2,1,0:T(8,128)(2,1)S(1)}, bf16[1,480,128]{2,1,0:T(8,128)(2,1)S(1)}, u32[]{:S(2)}, u32[]{:S(2)}) %collective-permute-start) | collective-permute-done | bytes 122912 | tf_op jit(solution)/shard_map/ppermute | solution.py:423
  37.6 0.7 %shard_map.44 = bf16[40,16,6,2,128]{4,3,2,1,0:T(2,128)(2,1)} custom-call(bf16[1,40,6,2,128]{4,3,2,1,0:T(2,128)(2,1)S(1)} %bitcast.18, bf16[40,16,6,2,128]{4,3,2,1,0:T(2,128)(2,1)} %shard_map.43.refs_1_), custom_call_target="tpu_custom_call", output_to_operand_aliasing={{}: (1, {})} | custom-call | tf_op jit(solution)/shard_map/pallas_call | solution.py:305
Async XLA Ops:
  0.0 3.6 %copy-start = (s32[8]{0:T(128)S(1)}, s32[8]{0:T(128)}, u32[]{:S(2)}) copy-start(s32[8]{0:T(128)} %pair_ref.3) | copy-start | bytes 100
  0.0 3.6 %copy-start.1 = (f32[640]{0:T(1024)S(1)}, f32[640]{0:T(1024)}, u32[]{:S(2)}) copy-start(f32[640]{0:T(1024)} %refs_1_.1) | copy-start | bytes 7684
  12.8 23.0 %collective-permute-start.4 = (bf16[2,480,128]{2,1,0:T(8,128)(2,1)S(1)}, bf16[2,480,128]{2,1,0:T(8,128)(2,1)S(1)}, u32[]{:S(2)}, u32[]{:S(2)}) collective-permute-start(bf16[2,480,128]{2,1,0:T(8,128)(2,1)S(1)} %get-tuple-element.26), channel_id=1, source_target_pairs={{0,1},{1,0},{2,3},{3,2},{4,5},{5,4},{6,7},{7,6},{8,9},{9,8},{10,11... | collective-permute-start | bytes 737288 | tf_op jit(solution)/shard_map/ppermute | solution.py:423
  15.9 20.0 %collective-permute-start.3 = (bf16[2,480,128]{2,1,0:T(8,128)(2,1)S(1)}, bf16[2,480,128]{2,1,0:T(8,128)(2,1)S(1)}, u32[]{:S(2)}, u32[]{:S(2)}) collective-permute-start(bf16[2,480,128]{2,1,0:T(8,128)(2,1)S(1)} %get-tuple-element.25), channel_id=1, source_target_pairs={{0,1},{1,0},{2,3},{3,2},{4,5},{5,4},{6,7},{7,6},{8,9},{9,8},{10,11... | collective-permute-start | bytes 737288 | tf_op jit(solution)/shard_map/ppermute | solution.py:423
  17.4 18.5 %collective-permute-start.2 = (bf16[2,480,128]{2,1,0:T(8,128)(2,1)S(1)}, bf16[2,480,128]{2,1,0:T(8,128)(2,1)S(1)}, u32[]{:S(2)}, u32[]{:S(2)}) collective-permute-start(bf16[2,480,128]{2,1,0:T(8,128)(2,1)S(1)} %shard_map.42), channel_id=1, source_target_pairs={{0,1},{1,0},{2,3},{3,2},{4,5},{5,4},{6,7},{7,6},{8,9},{9,8},{10,11... | collective-permute-start | bytes 737288 | tf_op jit(solution)/shard_map/ppermute | solution.py:423
  19.4 16.5 %collective-permute-start.1 = (bf16[1,480,128]{2,1,0:T(8,128)(2,1)S(1)}, bf16[1,480,128]{2,1,0:T(8,128)(2,1)S(1)}, u32[]{:S(2)}, u32[]{:S(2)}) collective-permute-start(bf16[1,480,128]{2,1,0:T(8,128)(2,1)S(1)} %get-tuple-element.24), channel_id=1, source_target_pairs={{0,1},{1,0},{2,3},{3,2},{4,5},{5,4},{6,7},{7,6},{8,9},{9,8},{10,11... | collective-permute-start | bytes 368648 | tf_op jit(solution)/shard_map/ppermute | solution.py:423
  22.2 15.4 %collective-permute-start = (bf16[1,480,128]{2,1,0:T(8,128)(2,1)S(1)}, bf16[1,480,128]{2,1,0:T(8,128)(2,1)S(1)}, u32[]{:S(2)}, u32[]{:S(2)}) collective-permute-start(bf16[1,480,128]{2,1,0:T(8,128)(2,1)S(1)} %get-tuple-element.19), channel_id=1, source_target_pairs={{0,1},{1,0},{2,3},{3,2},{4,5},{5,4},{6,7},{7,6},{8,9},{9,8},{10,11... | collective-permute-start | bytes 368648 | tf_op jit(solution)/shard_map/ppermute | solution.py:423

commit v5 on v4

--- a/solution.py
+++ b/solution.py
@@ -13,6 +13,7 @@
 F32 = jnp.float32
 BF16 = jnp.bfloat16
 CHUNKS = (1, 2, 2, 2, 1)
+LATE = 2
 AHEAD = 2
 PIECES = 4
 VMEM = pl.BlockSpec(memory_space=pltpu.VMEM)
@@ -143,19 +144,32 @@
         tile = p_ref[pl.ds(block * LANES * pitch + h, n, stride=pitch), :]
         pt_ref[pl.ds(h * LANES, LANES), pl.ds(block * LANES, n)] = tile.T
 
-    for block in range(lay.blocks):
-        n = min(LANES, lay.slots - block * LANES)
-        for i in range(n):
-            slot = block * LANES + i
-            if i == LANES // 8 and block + 1 < lay.blocks and table is not None:
-                table(block + 1)
-            if block and i >= LANES // 4 and (i - LANES // 4) % 8 == 0 and (i - LANES // 4) // 8 < high and n == LANES:
-                turn(block - 1, (i - LANES // 4) // 8)
-            a, b, g = (coef_ref[c, pl.ds(slot, 1), :] for c in range(3))
-            tail = jnp.where(switch == slot, seed2, g * before) if slot >= 2 else g * before
-            now = (a * x2 - b) * last - tail
-            p_ref[pl.ds(slot * pitch, high), :] = now
-            last, before = now, last
+    earliest = (M - (M // 2 - 1)) // 2
+
+    def coef(slot):
+        a, b, g = (coef_ref[c, pl.ds(slot, 1), :] for c in range(3))
+        return a * x2 - b, g
+
+    def keep(slot, value):
+        p_ref[pl.ds(slot * pitch, high), :] = value
+
+    for slot in range(0, lay.slots, 2):
+        block, i = divmod(slot, LANES)
+        if table is not None and i == LANES // 8 and block + 1 < lay.blocks:
+            table(block + 1)
+        if block and i >= LANES // 4 and (i - LANES // 4) % 8 == 0 and (i - LANES // 4) // 8 < high:
+            turn(block - 1, (i - LANES // 4) // 8)
+        (c1, g1), (c2, g2) = coef(slot), coef(slot + 1)
+        one = c1 * last - g1 * before
+        two = (c2 * c1 - g2) * last
+        if slot + 1 >= earliest:
+            skip1 = jnp.where(switch == slot, seed2, 0.0)
+            one = one - skip1
+            two = two - (c2 * skip1 + jnp.where(switch == slot + 1, seed2, 0.0))
+        two = two - (c2 * g1) * before
+        keep(slot, one)
+        keep(slot + 1, two)
+        last, before = two, one
     whole = lay.slots // LANES
     for block in range(whole - 1, lay.blocks):
         for h in range(high):
@@ -188,27 +202,27 @@
         out_ref[...] = stage_ref[...].astype(BF16)
 
 
-def fetches(lay, spec_ref, buf_ref, sems, begin, n):
+def fetches(lay, spec_ref, buf_ref, sems, begin, i):
     step = lay.slots // PIECES // 16 * 16
     edges = [step * k for k in range(PIECES)] + [lay.slots]
     return [
-        [
-            pltpu.make_async_copy(
-                spec_ref.at[begin + i, q, pl.ds(edges[k], edges[k + 1] - edges[k])],
-                buf_ref.at[i, q, pl.ds(edges[k], edges[k + 1] - edges[k])],
-                sems.at[i, q, k],
-            )
-            for q in range(2)
-            for k in range(PIECES)
-        ]
-        for i in range(n)
+        pltpu.make_async_copy(
+            spec_ref.at[begin + i, q, pl.ds(edges[k], edges[k + 1] - edges[k])],
+            buf_ref.at[i, q, pl.ds(edges[k], edges[k + 1] - edges[k])],
+            sems.at[i, q, k],
+        )
+        for q in range(2)
+        for k in range(PIECES)
     ]
 
 
-def begin_all(copies):
-    for group in copies:
-        for copy in group:
+def begin_all(lay, spec_ref, buf_ref, sems, begin, n):
+    def begin_set(i, carry):
+        for copy in fetches(lay, spec_ref, buf_ref, sems, begin, i):
             copy.start()
+        return carry
+
+    lax.fori_loop(0, n, begin_set, 0)
 
 
 def wait_all(copies):
@@ -227,12 +241,11 @@
     *, lay, n, count, offset,
 ):
     kept = buf_ref.shape[0]
-    copies = fetches(lay, spec_ref, buf_ref, sems, 0, kept)
     pair_copy = pltpu.make_async_copy(pair_hbm, pair_ref, small.at[0])
     sines_copy = pltpu.make_async_copy(sines_hbm, sines_ref, small.at[1])
     pair_copy.start()
     sines_copy.start()
-    begin_all(copies)
+    begin_all(lay, spec_ref, buf_ref, sems, 0, kept)
     sign, band, ma = position()
     pair_copy.wait()
     table_block(lay, pair_ref, tab_ref, coef_ref, 0)
@@ -243,7 +256,7 @@
         lambda block: table_block(lay, pair_ref, tab_ref, coef_ref, block),
     )
     for i in range(kept):
-        wait_all(copies[i])
+        wait_all(fetches(lay, spec_ref, buf_ref, sems, 0, i))
         if i < n:
             project(lay, pair_ref, [(pt_ref, count, stage_ref, out_ref.at[i])], buf_ref.at[i], i)
 
@@ -267,8 +280,7 @@
     if make:
         own_pt_ref = refs.pop(0)
     buf_ref, stage_ref, sems = refs.pop(0), refs.pop(0), refs.pop(0)
-    copies = fetches(lay, spec_ref, buf_ref, sems, begin, n)
-    begin_all(copies)
+    begin_all(lay, spec_ref, buf_ref, sems, begin, n)
     if lay.split:
         own_stage_ref = refs.pop(0)
     if make:
@@ -277,7 +289,7 @@
         x = gather_rows(lay, sines_ref, band * lay.band, ma * lay.own, lay.own)
         legendre(lay, pair_ref, sign, x, coef_ref, p_ref, own_pt_ref, lay.own, None)
     for i in range(n):
-        wait_all(copies[i])
+        wait_all(fetches(lay, spec_ref, buf_ref, sems, begin, i))
         groups = [(pt_ref, count, stage_ref, out_ref.at[i])]
         if lay.split:
             groups.append((own_pt_ref, lay.own, own_stage_ref, own_ref.at[i]))
@@ -421,7 +433,7 @@
             mine.append((parts[:, 0], begins[k]))
         for d in range(1, peers):
             moved = lax.ppermute(parts[:, first_peer + d - 1], "ma", [(i, (i + d) % peers) for i in range(peers)])
-            (late if k == len(CHUNKS) - 1 else early).append((moved.reshape(n, own, cb, 2, LANES), (d, begins[k])))
+            (late if k >= len(CHUNKS) - LATE else early).append((moved.reshape(n, own, cb, 2, LANES), (d, begins[k])))
     if split:
         (first_own,) = call(
             functools.partial(kept_kernel, lay=lay, begin=0, count=own),

time: 38.4 us -> 32.9 us (0.86)
  waiting for transfers between devices: 10.2 us -> 6.55 us
  Pallas kernels: 20.8 us -> 18.8 us
    ppermute x5, waiting for transfers between devices: 10.2 us -> 6.55 us  [transform(): lax.ppermute(parts[:, first_peer + d - 1], 'ma', [(i, (i + d) % peers) fo...]
    pallas_call x6, Pallas kernels: 18.7 us -> 16.8 us  [call(): pl.pallas_call(kernel, in_specs=in_specs, out_specs=[VMEM] * len(shapes),...]
  transfers between devices with their start and end apart: 5 -> 5, of which waited for: 2 -> 2; matrix products, arithmetic and copies ran while one was open for 0% -> 0% of each run, Pallas kernels for 19% -> 33%
where the time goes in v5:
time: 32.9 us; the launch traced here: 32.7 us
  Pallas kernels  18.8 us (57%)
  starting transfers between devices  7.28 us (22%)
  waiting for transfers between devices  6.55 us (20%)
    pallas_call x6, Pallas kernels, call(): pl.pallas_call(kernel, in_specs=in_specs, out_specs=[VMEM] * len(shapes),...  16.8 us
    ppermute x5, starting transfers between devices, transform(): lax.ppermute(parts[:, first_peer + d - 1], 'ma', [(i, (i + d) % peers) fo...  7.28 us
    ppermute x5, waiting for transfers between devices, transform(): lax.ppermute(parts[:, first_peer + d - 1], 'ma', [(i, (i + d) % peers) fo...  6.55 us
    pallas_call x2, Pallas kernels, place(): pl.pallas_call(functools.partial(place_kernel, plan=plan, sets=sets, peer...  2 us
  transfers between devices with their start and end apart: 5, of which 2 were waited for; matrix products, arithmetic and copies ran while one was open for 0% of the time, Pallas kernels for 33%

profile of v5, /device:TPU:0, one launch (start us, length us, event | category | flops | bytes accessed | tf_op | source)
XLA Modules:
  0.0 32.7 jit_solution(13355869311045525458)
XLA Ops:
  0.0 0.0 copy-start
  0.0 0.0 copy-start.1
  0.0 3.4 %shard_map.37 = (bf16[1,480,128]{2,1,0:T(8,128)(2,1)S(1)}, f32[640,768]{1,0:T(8,128)S(1)}, f32[3,768,128]{2,1,0:T(8,128)S(1)}, bf16[3,2,648,768]{3,2,1,0:T(8,128)(2,1)S(1)}) custom-call(s32[8]{0:T(128)} %pair_ref.3, f32[640]{0:T(1024)} %refs_1_.1, bf16[8,2,648,768]{3,2,1,0:T(8,128)(2,1)} %refs_3_.3), custom_call_target="tpu_custom_call" | custom-call | tf_op jit(solution)/shard_map/pallas_call | solution.py:357
  3.4 0.0 copy-done
  3.4 0.0 copy-done.1
  3.4 3.8 %shard_map.38 = (bf16[2,480,128]{2,1,0:T(8,128)(2,1)S(1)}, bf16[2,480,128]{2,1,0:T(8,128)(2,1)S(1)}, f32[640,768]{1,0:T(8,128)S(1)}) custom-call(s32[8]{0:T(128)S(1)} %copy-done, f32[640]{0:T(1024)S(1)} %copy-done.1, f32[3,768,128]{2,1,0:T(8,128)S(1)} %get-tuple-element.17.refs_2_, f32[640,768]{1,0:T(8,128)S(1)} %get-tuple-element.16.refs_3_.refs_1_.pt_ref, ...), custom_call_target="tpu_custom_call" | custom-call | tf_op jit(solution)/shard_map/pallas_call | solution.py:357
  7.2 3.0 %collective-permute-start.4 = (bf16[2,480,128]{2,1,0:T(8,128)(2,1)S(1)}, bf16[2,480,128]{2,1,0:T(8,128)(2,1)S(1)}, u32[]{:S(2)}, u32[]{:S(2)}) collective-permute-start(bf16[2,480,128]{2,1,0:T(8,128)(2,1)S(1)} %get-tuple-element.26), channel_id=1, source_target_pairs={{0,1},{1,0},{2,3},{3,2},{4,5},{5,4},{6,7},{7,6},{8,9},{9,8},{10,11... | collective-permute-start | bytes 737288 | tf_op jit(solution)/shard_map/ppermute | solution.py:435
  10.2 1.4 %shard_map.42 = bf16[2,480,128]{2,1,0:T(8,128)(2,1)S(1)} custom-call(s32[8]{0:T(128)S(1)} %copy-done, f32[640,768]{1,0:T(8,128)S(1)} %get-tuple-element.16.refs_3_.refs_1_.pt_ref, bf16[3,2,648,768]{3,2,1,0:T(8,128)(2,1)S(1)} %get-tuple-element.24.buf_ref), custom_call_target="tpu_custom_call" | custom-call | tf_op jit(solution)/shard_map/pallas_call | solution.py:357
  11.6 0.1 collective-permute-start.3
  11.7 3.7 %shard_map.39 = (bf16[2,480,128]{2,1,0:T(8,128)(2,1)S(1)}, bf16[2,480,128]{2,1,0:T(8,128)(2,1)S(1)}) custom-call(s32[8]{0:T(128)S(1)} %copy-done, f32[640,768]{1,0:T(8,128)S(1)} %get-tuple-element.16.refs_3_.refs_1_.pt_ref, f32[640,768]{1,0:T(8,128)S(1)} %get-tuple-element.18.refs_2_.pt_ref, bf16[8,2,648,768]{3,2,1,0:T(8,128)(2,1)} %refs_3_.3), custom_call_target="tpu_custom_call" | custom-call | tf_op jit(solution)/shard_map/pallas_call | solution.py:357
  15.4 2.1 %collective-permute-start = (bf16[2,480,128]{2,1,0:T(8,128)(2,1)S(1)}, bf16[2,480,128]{2,1,0:T(8,128)(2,1)S(1)}, u32[]{:S(2)}, u32[]{:S(2)}) collective-permute-start(bf16[2,480,128]{2,1,0:T(8,128)(2,1)S(1)} %get-tuple-element.19), channel_id=1, source_target_pairs={{0,1},{1,0},{2,3},{3,2},{4,5},{5,4},{6,7},{7,6},{8,9},{9,8},{10,11... | collective-permute-start | bytes 737288 | tf_op jit(solution)/shard_map/ppermute | solution.py:435
  17.5 0.1 collective-permute-start.2
  17.6 2.8 %shard_map.40 = (bf16[1,480,128]{2,1,0:T(8,128)(2,1)S(1)}, bf16[1,480,128]{2,1,0:T(8,128)(2,1)S(1)}) custom-call(s32[8]{0:T(128)S(1)} %copy-done, f32[640,768]{1,0:T(8,128)S(1)} %get-tuple-element.16.refs_3_.refs_1_.pt_ref, f32[640,768]{1,0:T(8,128)S(1)} %get-tuple-element.18.refs_2_.pt_ref, bf16[8,2,648,768]{3,2,1,0:T(8,128)(2,1)} %refs_3_.3), custom_call_target="tpu_custom_call" | custom-call | tf_op jit(solution)/shard_map/pallas_call | solution.py:357
  20.3 2.0 %collective-permute-start.1 = (bf16[1,480,128]{2,1,0:T(8,128)(2,1)S(1)}, bf16[1,480,128]{2,1,0:T(8,128)(2,1)S(1)}, u32[]{:S(2)}, u32[]{:S(2)}) collective-permute-start(bf16[1,480,128]{2,1,0:T(8,128)(2,1)S(1)} %get-tuple-element.20), channel_id=1, source_target_pairs={{0,1},{1,0},{2,3},{3,2},{4,5},{5,4},{6,7},{7,6},{8,9},{9,8},{10,11... | collective-permute-start | bytes 368648 | tf_op jit(solution)/shard_map/ppermute | solution.py:435
  22.4 1.8 %shard_map.41 = bf16[3,480,128]{2,1,0:T(8,128)(2,1)S(1)} custom-call(s32[8]{0:T(128)S(1)} %copy-done, f32[640,768]{1,0:T(8,128)S(1)} %get-tuple-element.18.refs_2_.pt_ref, bf16[3,2,648,768]{3,2,1,0:T(8,128)(2,1)S(1)} %get-tuple-element.24.buf_ref), custom_call_target="tpu_custom_call" | custom-call | tf_op jit(solution)/shard_map/pallas_call | solution.py:357
  24.1 6.0 %collective-permute-done.2 = bf16[1,480,128]{2,1,0:T(8,128)(2,1)S(1)} collective-permute-done((bf16[1,480,128]{2,1,0:T(8,128)(2,1)S(1)}, bf16[1,480,128]{2,1,0:T(8,128)(2,1)S(1)}, u32[]{:S(2)}, u32[]{:S(2)}) %collective-permute-start.2) | collective-permute-done | bytes 122912 | tf_op jit(solution)/shard_map/ppermute | solution.py:435
  30.2 0.0 collective-permute-done.4
  30.2 0.0 collective-permute-done.3
  30.2 1.2 %shard_map.43.refs_2_ = bf16[40,16,6,2,128]{4,3,2,1,0:T(2,128)(2,1)} custom-call(bf16[2,40,6,2,128]{4,3,2,1,0:T(2,128)(2,1)S(1)} %bitcast.13, bf16[2,40,6,2,128]{4,3,2,1,0:T(2,128)(2,1)S(1)} %bitcast.17, bf16[1,40,6,2,128]{4,3,2,1,0:T(2,128)(2,1)S(1)} %bitcast.19, bf16[3,40,6,2,128]{4,3,2,1,0:T(2,128)(2,1)S(1)} %bitcast.12, ...), custom_call_target="tpu_custom_call" | custom-call | tf_op jit(solution)/shard_map/pallas_call | solution.py:317
  31.4 0.5 %collective-permute-done.1 = bf16[1,480,128]{2,1,0:T(8,128)(2,1)S(1)} collective-permute-done((bf16[1,480,128]{2,1,0:T(8,128)(2,1)S(1)}, bf16[1,480,128]{2,1,0:T(8,128)(2,1)S(1)}, u32[]{:S(2)}, u32[]{:S(2)}) %collective-permute-start.1) | collective-permute-done | bytes 122912 | tf_op jit(solution)/shard_map/ppermute | solution.py:435
  31.9 0.0 collective-permute-done
  32.0 0.8 %shard_map.44 = bf16[40,16,6,2,128]{4,3,2,1,0:T(2,128)(2,1)} custom-call(bf16[2,40,6,2,128]{4,3,2,1,0:T(2,128)(2,1)S(1)} %bitcast.14, bf16[1,40,6,2,128]{4,3,2,1,0:T(2,128)(2,1)S(1)} %bitcast.20, bf16[40,16,6,2,128]{4,3,2,1,0:T(2,128)(2,1)} %shard_map.43.refs_2_), custom_call_target="tpu_custom_call", output_to_operand_aliasing={{}: (2, {})} | custom-call | tf_op jit(solution)/shard_map/pallas_call | solution.py:317
Async XLA Ops:
  0.0 3.4 %copy-start = (s32[8]{0:T(128)S(1)}, s32[8]{0:T(128)}, u32[]{:S(2)}) copy-start(s32[8]{0:T(128)} %pair_ref.3) | copy-start | bytes 100
  0.0 3.4 %copy-start.1 = (f32[640]{0:T(1024)S(1)}, f32[640]{0:T(1024)}, u32[]{:S(2)}) copy-start(f32[640]{0:T(1024)} %refs_1_.1) | copy-start | bytes 7684
  7.2 23.0 %collective-permute-start.4 = (bf16[2,480,128]{2,1,0:T(8,128)(2,1)S(1)}, bf16[2,480,128]{2,1,0:T(8,128)(2,1)S(1)}, u32[]{:S(2)}, u32[]{:S(2)}) collective-permute-start(bf16[2,480,128]{2,1,0:T(8,128)(2,1)S(1)} %get-tuple-element.26), channel_id=1, source_target_pairs={{0,1},{1,0},{2,3},{3,2},{4,5},{5,4},{6,7},{7,6},{8,9},{9,8},{10,11... | collective-permute-start | bytes 737288 | tf_op jit(solution)/shard_map/ppermute | solution.py:435
  11.6 18.6 %collective-permute-start.3 = (bf16[2,480,128]{2,1,0:T(8,128)(2,1)S(1)}, bf16[2,480,128]{2,1,0:T(8,128)(2,1)S(1)}, u32[]{:S(2)}, u32[]{:S(2)}) collective-permute-start(bf16[2,480,128]{2,1,0:T(8,128)(2,1)S(1)} %shard_map.42), channel_id=1, source_target_pairs={{0,1},{1,0},{2,3},{3,2},{4,5},{5,4},{6,7},{7,6},{8,9},{9,8},{10,11... | collective-permute-start | bytes 737288 | tf_op jit(solution)/shard_map/ppermute | solution.py:435
  15.4 16.6 %collective-permute-start = (bf16[2,480,128]{2,1,0:T(8,128)(2,1)S(1)}, bf16[2,480,128]{2,1,0:T(8,128)(2,1)S(1)}, u32[]{:S(2)}, u32[]{:S(2)}) collective-permute-start(bf16[2,480,128]{2,1,0:T(8,128)(2,1)S(1)} %get-tuple-element.19), channel_id=1, source_target_pairs={{0,1},{1,0},{2,3},{3,2},{4,5},{5,4},{6,7},{7,6},{8,9},{9,8},{10,11... | collective-permute-start | bytes 737288 | tf_op jit(solution)/shard_map/ppermute | solution.py:435
  17.5 12.7 %collective-permute-start.2 = (bf16[1,480,128]{2,1,0:T(8,128)(2,1)S(1)}, bf16[1,480,128]{2,1,0:T(8,128)(2,1)S(1)}, u32[]{:S(2)}, u32[]{:S(2)}) collective-permute-start(bf16[1,480,128]{2,1,0:T(8,128)(2,1)S(1)} %get-tuple-element.25), channel_id=1, source_target_pairs={{0,1},{1,0},{2,3},{3,2},{4,5},{5,4},{6,7},{7,6},{8,9},{9,8},{10,11... | collective-permute-start | bytes 368648 | tf_op jit(solution)/shard_map/ppermute | solution.py:435
  20.3 11.6 %collective-permute-start.1 = (bf16[1,480,128]{2,1,0:T(8,128)(2,1)S(1)}, bf16[1,480,128]{2,1,0:T(8,128)(2,1)S(1)}, u32[]{:S(2)}, u32[]{:S(2)}) collective-permute-start(bf16[1,480,128]{2,1,0:T(8,128)(2,1)S(1)} %get-tuple-element.20), channel_id=1, source_target_pairs={{0,1},{1,0},{2,3},{3,2},{4,5},{5,4},{6,7},{7,6},{8,9},{9,8},{10,11... | collective-permute-start | bytes 368648 | tf_op jit(solution)/shard_map/ppermute | solution.py:435

commit v6 on v5

--- a/solution.py
+++ b/solution.py
@@ -15,7 +15,7 @@
 CHUNKS = (1, 2, 2, 2, 1)
 LATE = 2
 AHEAD = 2
-PIECES = 4
+PIECES = 1
 VMEM = pl.BlockSpec(memory_space=pltpu.VMEM)
 SMEM = pl.BlockSpec(memory_space=pltpu.SMEM)
 ANY = pl.BlockSpec(memory_space=pl.ANY)
@@ -142,7 +142,8 @@
     def turn(block, h):
         n = min(LANES, lay.slots - block * LANES)
         tile = p_ref[pl.ds(block * LANES * pitch + h, n, stride=pitch), :]
-        pt_ref[pl.ds(h * LANES, LANES), pl.ds(block * LANES, n)] = tile.T
+        tile = tile.astype(BF16).T if n == LANES else tile.T.astype(BF16)
+        pt_ref[pl.ds(h * LANES, LANES), pl.ds(block * LANES, n)] = tile
 
     earliest = (M - (M // 2 - 1)) // 2
 
@@ -155,8 +156,10 @@
 
     for slot in range(0, lay.slots, 2):
         block, i = divmod(slot, LANES)
-        if table is not None and i == LANES // 8 and block + 1 < lay.blocks:
-            table(block + 1)
+        if table is not None and i == LANES // 8:
+            for ahead in (1, 2) if block == 0 else (2,):
+                if block + ahead < lay.blocks:
+                    table(block + ahead)
         if block and i >= LANES // 4 and (i - LANES // 4) % 8 == 0 and (i - LANES // 4) // 8 < high:
             turn(block - 1, (i - LANES // 4) // 8)
         (c1, g1), (c2, g2) = coef(slot), coef(slot + 1)
@@ -176,18 +179,23 @@
             turn(block, h)
 
 
-def project(lay, pair_ref, groups, spec, s):
+def project(lay, pairs_ref, groups, spec, s):
     acc = None
-    pair = pair_ref[s]
+    pair = pairs_ref[pl.ds(s, 1), pl.ds(0, lay.slots)]
     here = pl.ds(0, lay.slots)
     for q in range(2):
         base = (q * lay.sets + s) * lay.low
         parts = []
         for pt_ref, count, _, _ in groups:
+            pair_base, half = divmod(base, 2 * lay.low)
             w = jnp.concatenate(
-                [pt_ref[pl.ds(h * LANES + base, lay.low), here] for h in range(lay.high(count))], axis=0
+                [
+                    pt_ref[pl.ds(h * LANES + pair_base * 2 * lay.low, 2 * lay.low), here].astype(F32)[half : half + lay.low]
+                    for h in range(lay.high(count))
+                ],
+                axis=0,
             )
-            first = lax.broadcasted_iota(jnp.int32, (count, lay.slots), 1) < (M - pair + 1 - q) // 2
+            first = lax.broadcasted_iota(jnp.int32, (count, lay.slots), 1) < lax.shift_right_logical(M - pair + 1 - q, 1)
             parts += [jnp.where(first, w, 0.0), jnp.where(first, 0.0, w)]
         part = jnp.dot(jnp.concatenate(parts, axis=0).astype(BF16), spec[q], preferred_element_type=F32)
         acc = part if acc is None else acc + part
@@ -237,7 +245,7 @@
 
 
 def head_kernel(
-    pair_hbm, sines_hbm, spec_ref, out_ref, pt_ref, coef_ref, buf_ref, pair_ref, sines_ref, tab_ref, p_ref, stage_ref, small, sems,
+    pair_hbm, sines_hbm, spec_ref, out_ref, pt_ref, coef_ref, buf_ref, pairs_ref, pair_ref, sines_ref, tab_ref, p_ref, stage_ref, small, sems,
     *, lay, n, count, offset,
 ):
     kept = buf_ref.shape[0]
@@ -248,8 +256,10 @@
     begin_all(lay, spec_ref, buf_ref, sems, 0, kept)
     sign, band, ma = position()
     pair_copy.wait()
+    sines_copy.wait()
+    for s in range(lay.sets):
+        pairs_ref[pl.ds(s, 1), :] = jnp.full((1, lay.padded), pair_ref[s], jnp.int32)
     table_block(lay, pair_ref, tab_ref, coef_ref, 0)
-    sines_copy.wait()
     x = gather_rows(lay, sines_ref, band * lay.band, ma * lay.own + offset, count)
     legendre(
         lay, pair_ref, sign, x, coef_ref, p_ref, pt_ref, count,
@@ -258,19 +268,19 @@
     for i in range(kept):
         wait_all(fetches(lay, spec_ref, buf_ref, sems, 0, i))
         if i < n:
-            project(lay, pair_ref, [(pt_ref, count, stage_ref, out_ref.at[i])], buf_ref.at[i], i)
-
-
-def kept_kernel(pair_ref, pt_ref, buf_ref, out_ref, stage_ref, *, lay, begin, count):
+            project(lay, pairs_ref, [(pt_ref, count, stage_ref, out_ref.at[i])], buf_ref.at[i], i)
+
+
+def kept_kernel(pairs_ref, pt_ref, buf_ref, out_ref, stage_ref, *, lay, begin, count):
     for i in range(out_ref.shape[0]):
-        project(lay, pair_ref, [(pt_ref, count, stage_ref, out_ref.at[i])], buf_ref.at[begin + i], begin + i)
+        project(lay, pairs_ref, [(pt_ref, count, stage_ref, out_ref.at[i])], buf_ref.at[begin + i], begin + i)
 
 
 def late_kernel(*refs, lay, n, begin, count, make):
     refs = list(refs)
-    pair_ref = refs.pop(0)
+    pairs_ref = refs.pop(0)
     if make:
-        sines_ref, coef_ref = refs.pop(0), refs.pop(0)
+        pair_ref, sines_ref, coef_ref = refs.pop(0), refs.pop(0), refs.pop(0)
     pt_ref = refs.pop(0)
     if lay.split and not make:
         own_pt_ref = refs.pop(0)
@@ -293,7 +303,7 @@
         groups = [(pt_ref, count, stage_ref, out_ref.at[i])]
         if lay.split:
             groups.append((own_pt_ref, lay.own, own_stage_ref, own_ref.at[i]))
-        project(lay, pair_ref, groups, buf_ref.at[i], begin + i)
+        project(lay, pairs_ref, groups, buf_ref.at[i], begin + i)
 
 
 def place_kernel(*refs, plan, sets, peers):
@@ -337,9 +347,11 @@
     cb = lay.cb
 
     split = lay.split
-    pt_shape = jax.ShapeDtypeStruct((lay.high(count) * LANES, lay.padded), F32)
-    own_pt_shape = jax.ShapeDtypeStruct((lay.high(own) * LANES, lay.padded), F32)
+    pt_shape = jax.ShapeDtypeStruct((lay.high(count) * LANES, lay.padded), BF16)
+    own_pt_shape = jax.ShapeDtypeStruct((lay.high(own) * LANES, lay.padded), BF16)
     coef_shape = jax.ShapeDtypeStruct((3, lay.padded, LANES), F32)
+
+    pairs_shape = jax.ShapeDtypeStruct((sets, lay.padded), jnp.int32)
 
     def p_scratch(rows):
         return pltpu.VMEM((lay.padded * lay.pitch(rows), LANES), F32)
@@ -368,10 +380,10 @@
     made, mine = [], []
     for k, n in enumerate(CHUNKS):
         if k == 0:
-            sent, pt, coef, buf = call(
+            sent, pt, coef, buf, pairs = call(
                 functools.partial(head_kernel, lay=lay, n=n, count=count, offset=offset),
                 [HBM] * 3,
-                [out_shape(n, count), pt_shape, coef_shape, jax.ShapeDtypeStruct((kept, 2, slots, cols), BF16)],
+                [out_shape(n, count), pt_shape, coef_shape, jax.ShapeDtypeStruct((kept, 2, slots, cols), BF16), pairs_shape],
                 [
                     pltpu.SMEM(set_pair.shape, jnp.int32),
                     pltpu.SMEM(lat_sines.shape, F32),
@@ -386,16 +398,16 @@
         elif k < AHEAD:
             (sent,) = call(
                 functools.partial(kept_kernel, lay=lay, begin=begins[k], count=count),
-                [SMEM, VMEM, VMEM],
+                [VMEM, VMEM, VMEM],
                 [out_shape(n, count)],
                 [stage(count)],
-                [set_pair, pt, buf],
+                [pairs, pt, buf],
             )
         else:
             make = split and k == AHEAD
-            operands = [(SMEM, set_pair)]
+            operands = [(VMEM, pairs)]
             if make:
-                operands += [(SMEM, lat_sines), (VMEM, coef)]
+                operands += [(SMEM, set_pair), (SMEM, lat_sines), (VMEM, coef)]
             operands.append((VMEM, pt))
             if split and not make:
                 operands.append((VMEM, own_pt))
@@ -427,26 +439,28 @@
         made.append(sent.reshape(n, count // own, own * lay.per_row, LANES))
 
     first_peer = 0 if split else 1
-    early, late = [], []
+    early, late = [], [[] for _ in range(LATE)]
     for k, (n, parts) in enumerate(zip(CHUNKS, made)):
         if not split:
             mine.append((parts[:, 0], begins[k]))
         for d in range(1, peers):
             moved = lax.ppermute(parts[:, first_peer + d - 1], "ma", [(i, (i + d) % peers) for i in range(peers)])
-            (late if k >= len(CHUNKS) - LATE else early).append((moved.reshape(n, own, cb, 2, LANES), (d, begins[k])))
+            group = early if k < len(CHUNKS) - LATE else late[k - len(CHUNKS)]
+            group.append((moved.reshape(n, own, cb, 2, LANES), (d, begins[k])))
     if split:
         (first_own,) = call(
             functools.partial(kept_kernel, lay=lay, begin=0, count=own),
-            [SMEM, VMEM, VMEM],
+            [VMEM, VMEM, VMEM],
             [out_shape(kept, own)],
             [stage(own)],
-            [set_pair, own_pt, buf],
+            [pairs, own_pt, buf],
         )
         mine.append((first_own, 0))
     early = [(part.reshape(part.shape[0], own, cb, 2, LANES), (0, begin)) for part, begin in mine] + early
     shape = (own, peers * sets, cb, 2, LANES)
     out = place([p for p, _ in early], [w for _, w in early], shape, sets, peers)
-    out = place([p for p, _ in late], [w for _, w in late], shape, sets, peers, out)
+    for group in late:
+        out = place([p for p, _ in group], [w for _, w in group], shape, sets, peers, out)
     return out.transpose(0, 1, 3, 2, 4).reshape(own, peers * sets, 2, cols)
 
 

time: 32.9 us -> 32.4 us (0.985)
  Pallas kernels: 18.8 us -> 16.3 us
  waiting for transfers between devices: 6.55 us -> 8.6 us
    pallas_call x6, Pallas kernels: 16.8 us -> 13.7 us  [call(): pl.pallas_call(kernel, in_specs=in_specs, out_specs=[VMEM] * len(shapes),...]
    ppermute x5, waiting for transfers between devices: 6.55 us -> 8.6 us  [transform(): lax.ppermute(parts[:, first_peer + d - 1], 'ma', [(i, (i + d) % peers) fo...]
    pallas_call x2 -> x3, Pallas kernels: 2 us -> 2.64 us  [place(): pl.pallas_call(functools.partial(place_kernel, plan=plan, sets=sets, peer...]
  transfers between devices with their start and end apart: 5 -> 5, of which waited for: 2 -> 1; matrix products, arithmetic and copies ran while one was open for 0% -> 0% of each run, Pallas kernels for 33% -> 28%
where the time goes in v6:
time: 32.4 us; the launch traced here: 32.3 us
  Pallas kernels  16.3 us (50%)
  waiting for transfers between devices  8.6 us (27%)
  starting transfers between devices  7.28 us (22%)
    pallas_call x6, Pallas kernels, call(): pl.pallas_call(kernel, in_specs=in_specs, out_specs=[VMEM] * len(shapes),...  13.7 us
    ppermute x5, waiting for transfers between devices, transform(): lax.ppermute(parts[:, first_peer + d - 1], 'ma', [(i, (i + d) % peers) fo...  8.6 us
    ppermute x5, starting transfers between devices, transform(): lax.ppermute(parts[:, first_peer + d - 1], 'ma', [(i, (i + d) % peers) fo...  7.28 us
    pallas_call x3, Pallas kernels, place(): pl.pallas_call(functools.partial(place_kernel, plan=plan, sets=sets, peer...  2.64 us
  transfers between devices with their start and end apart: 5, of which 1 were waited for; matrix products, arithmetic and copies ran while one was open for 0% of the time, Pallas kernels for 28%

profile of v6, /device:TPU:0, one launch (start us, length us, event | category | flops | bytes accessed | tf_op | source)
XLA Modules:
  0.0 32.3 jit_solution(793548547577442520)
XLA Ops:
  0.0 0.0 copy-start.1
  0.0 0.0 copy-start
  0.0 3.0 %shard_map.37 = (bf16[1,480,128]{2,1,0:T(8,128)(2,1)S(1)}, bf16[640,768]{1,0:T(8,128)(2,1)S(1)}, f32[3,768,128]{2,1,0:T(8,128)S(1)}, bf16[3,2,648,768]{3,2,1,0:T(8,128)(2,1)S(1)}, s32[8,768]{1,0:T(8,128)S(1)}) custom-call(s32[8]{0:T(128)} %refs_1_.1, f32[640]{0:T(1024)} %refs_2_.1, bf16[8,2,648,768]{3,2,1,0:T(8,128)(2,1)} %refs_3_.3), custom_call_target="tpu_custom_call" | custom-call | tf_op jit(solution)/shard_map/pallas_call | solution.py:369
  3.0 0.0 copy-done.1
  3.1 0.0 copy-done
  3.1 3.5 %shard_map.38 = (bf16[2,480,128]{2,1,0:T(8,128)(2,1)S(1)}, bf16[2,480,128]{2,1,0:T(8,128)(2,1)S(1)}, bf16[640,768]{1,0:T(8,128)(2,1)S(1)}) custom-call(s32[8,768]{1,0:T(8,128)S(1)} %get-tuple-element.17.refs_0_.pairs_ref, s32[8]{0:T(128)S(1)} %copy-done.1, f32[640]{0:T(1024)S(1)} %copy-done, f32[3,768,128]{2,1,0:T(8,128)S(1)} %get-tuple-element.19.refs_3_, ...), custom_call_target="tpu_custom_call" | custom-call | tf_op jit(solution)/shard_map/pallas_call | solution.py:369
  6.6 3.0 %collective-permute-start.4 = (bf16[2,480,128]{2,1,0:T(8,128)(2,1)S(1)}, bf16[2,480,128]{2,1,0:T(8,128)(2,1)S(1)}, u32[]{:S(2)}, u32[]{:S(2)}) collective-permute-start(bf16[2,480,128]{2,1,0:T(8,128)(2,1)S(1)} %get-tuple-element.28), channel_id=1, source_target_pairs={{0,1},{1,0},{2,3},{3,2},{4,5},{5,4},{6,7},{7,6},{8,9},{9,8},{10,11... | collective-permute-start | bytes 737288 | tf_op jit(solution)/shard_map/ppermute | solution.py:447
  9.6 0.9 %shard_map.42 = bf16[2,480,128]{2,1,0:T(8,128)(2,1)S(1)} custom-call(s32[8,768]{1,0:T(8,128)S(1)} %get-tuple-element.17.refs_0_.pairs_ref, bf16[640,768]{1,0:T(8,128)(2,1)S(1)} %get-tuple-element.18.refs_4_.refs_1_.pt_ref, bf16[3,2,648,768]{3,2,1,0:T(8,128)(2,1)S(1)} %get-tuple-element.26.buf_ref), custom_call_target="tpu_custom_call" | custom-call | tf_op jit(solution)/shard_map/pallas_call | solution.py:369
  10.5 0.1 collective-permute-start.3
  10.6 2.9 %shard_map.40 = (bf16[2,480,128]{2,1,0:T(8,128)(2,1)S(1)}, bf16[2,480,128]{2,1,0:T(8,128)(2,1)S(1)}) custom-call(s32[8,768]{1,0:T(8,128)S(1)} %get-tuple-element.17.refs_0_.pairs_ref, bf16[640,768]{1,0:T(8,128)(2,1)S(1)} %get-tuple-element.18.refs_4_.refs_1_.pt_ref, bf16[640,768]{1,0:T(8,128)(2,1)S(1)} %get-tuple-element.20.refs_2_.pt_ref, ...), custom_call_target="tpu_custom_call" | custom-call | tf_op jit(solution)/shard_map/pallas_call | solution.py:369
  13.5 2.1 %collective-permute-start.1 = (bf16[2,480,128]{2,1,0:T(8,128)(2,1)S(1)}, bf16[2,480,128]{2,1,0:T(8,128)(2,1)S(1)}, u32[]{:S(2)}, u32[]{:S(2)}) collective-permute-start(bf16[2,480,128]{2,1,0:T(8,128)(2,1)S(1)} %get-tuple-element.22), channel_id=1, source_target_pairs={{0,1},{1,0},{2,3},{3,2},{4,5},{5,4},{6,7},{7,6},{8,9},{9,8},{10,11... | collective-permute-start | bytes 737288 | tf_op jit(solution)/shard_map/ppermute | solution.py:447
  15.6 0.1 collective-permute-start.2
  15.7 2.1 %shard_map.39 = (bf16[1,480,128]{2,1,0:T(8,128)(2,1)S(1)}, bf16[1,480,128]{2,1,0:T(8,128)(2,1)S(1)}) custom-call(s32[8,768]{1,0:T(8,128)S(1)} %get-tuple-element.17.refs_0_.pairs_ref, bf16[640,768]{1,0:T(8,128)(2,1)S(1)} %get-tuple-element.18.refs_4_.refs_1_.pt_ref, bf16[640,768]{1,0:T(8,128)(2,1)S(1)} %get-tuple-element.20.refs_2_.pt_ref, ...), custom_call_target="tpu_custom_call" | custom-call | tf_op jit(solution)/shard_map/pallas_call | solution.py:369
  17.8 2.0 %collective-permute-start = (bf16[1,480,128]{2,1,0:T(8,128)(2,1)S(1)}, bf16[1,480,128]{2,1,0:T(8,128)(2,1)S(1)}, u32[]{:S(2)}, u32[]{:S(2)}) collective-permute-start(bf16[1,480,128]{2,1,0:T(8,128)(2,1)S(1)} %get-tuple-element.21), channel_id=1, source_target_pairs={{0,1},{1,0},{2,3},{3,2},{4,5},{5,4},{6,7},{7,6},{8,9},{9,8},{10,11... | collective-permute-start | bytes 368648 | tf_op jit(solution)/shard_map/ppermute | solution.py:447
  19.8 1.2 %shard_map.41 = bf16[3,480,128]{2,1,0:T(8,128)(2,1)S(1)} custom-call(s32[8,768]{1,0:T(8,128)S(1)} %get-tuple-element.17.refs_0_.pairs_ref, bf16[640,768]{1,0:T(8,128)(2,1)S(1)} %get-tuple-element.20.refs_2_.pt_ref, bf16[3,2,648,768]{3,2,1,0:T(8,128)(2,1)S(1)} %get-tuple-element.26.buf_ref), custom_call_target="tpu_custom_call" | custom-call | tf_op jit(solution)/shard_map/pallas_call | solution.py:369
  21.0 8.6 %collective-permute-done.2 = bf16[1,480,128]{2,1,0:T(8,128)(2,1)S(1)} collective-permute-done((bf16[1,480,128]{2,1,0:T(8,128)(2,1)S(1)}, bf16[1,480,128]{2,1,0:T(8,128)(2,1)S(1)}, u32[]{:S(2)}, u32[]{:S(2)}) %collective-permute-start.2) | collective-permute-done | bytes 122912 | tf_op jit(solution)/shard_map/ppermute | solution.py:447
  29.6 0.0 collective-permute-done.4
  29.6 0.0 collective-permute-done.3
  29.6 1.2 %shard_map.43.refs_1_ = bf16[40,16,6,2,128]{4,3,2,1,0:T(2,128)(2,1)} custom-call(bf16[2,40,6,2,128]{4,3,2,1,0:T(2,128)(2,1)S(1)} %bitcast.13, bf16[2,40,6,2,128]{4,3,2,1,0:T(2,128)(2,1)S(1)} %bitcast.17, bf16[1,40,6,2,128]{4,3,2,1,0:T(2,128)(2,1)S(1)} %bitcast.19, bf16[3,40,6,2,128]{4,3,2,1,0:T(2,128)(2,1)S(1)} %bitcast.12, ...), custom_call_target="tpu_custom_call" | custom-call | tf_op jit(solution)/shard_map/pallas_call | solution.py:327
  30.9 0.0 collective-permute-done.1
  30.9 0.7 %shard_map.44.refs_1_ = bf16[40,16,6,2,128]{4,3,2,1,0:T(2,128)(2,1)} custom-call(bf16[2,40,6,2,128]{4,3,2,1,0:T(2,128)(2,1)S(1)} %bitcast.15, bf16[40,16,6,2,128]{4,3,2,1,0:T(2,128)(2,1)} %shard_map.43.refs_1_), custom_call_target="tpu_custom_call", output_to_operand_aliasing={{}: (1, {})} | custom-call | tf_op jit(solution)/shard_map/pallas_call | solution.py:327
  31.6 0.0 collective-permute-done
  31.6 0.7 %shard_map.45 = bf16[40,16,6,2,128]{4,3,2,1,0:T(2,128)(2,1)} custom-call(bf16[1,40,6,2,128]{4,3,2,1,0:T(2,128)(2,1)S(1)} %bitcast.20, bf16[40,16,6,2,128]{4,3,2,1,0:T(2,128)(2,1)} %shard_map.44.refs_1_), custom_call_target="tpu_custom_call", output_to_operand_aliasing={{}: (1, {})} | custom-call | tf_op jit(solution)/shard_map/pallas_call | solution.py:327
Async XLA Ops:
  0.0 3.0 %copy-start.1 = (s32[8]{0:T(128)S(1)}, s32[8]{0:T(128)}, u32[]{:S(2)}) copy-start(s32[8]{0:T(128)} %refs_1_.1) | copy-start | bytes 100
  0.0 3.1 %copy-start = (f32[640]{0:T(1024)S(1)}, f32[640]{0:T(1024)}, u32[]{:S(2)}) copy-start(f32[640]{0:T(1024)} %refs_2_.1) | copy-start | bytes 7684
  6.6 23.0 %collective-permute-start.4 = (bf16[2,480,128]{2,1,0:T(8,128)(2,1)S(1)}, bf16[2,480,128]{2,1,0:T(8,128)(2,1)S(1)}, u32[]{:S(2)}, u32[]{:S(2)}) collective-permute-start(bf16[2,480,128]{2,1,0:T(8,128)(2,1)S(1)} %get-tuple-element.28), channel_id=1, source_target_pairs={{0,1},{1,0},{2,3},{3,2},{4,5},{5,4},{6,7},{7,6},{8,9},{9,8},{10,11... | collective-permute-start | bytes 737288 | tf_op jit(solution)/shard_map/ppermute | solution.py:447
  10.5 19.1 %collective-permute-start.3 = (bf16[2,480,128]{2,1,0:T(8,128)(2,1)S(1)}, bf16[2,480,128]{2,1,0:T(8,128)(2,1)S(1)}, u32[]{:S(2)}, u32[]{:S(2)}) collective-permute-start(bf16[2,480,128]{2,1,0:T(8,128)(2,1)S(1)} %shard_map.42), channel_id=1, source_target_pairs={{0,1},{1,0},{2,3},{3,2},{4,5},{5,4},{6,7},{7,6},{8,9},{9,8},{10,11... | collective-permute-start | bytes 737288 | tf_op jit(solution)/shard_map/ppermute | solution.py:447
  13.5 17.3 %collective-permute-start.1 = (bf16[2,480,128]{2,1,0:T(8,128)(2,1)S(1)}, bf16[2,480,128]{2,1,0:T(8,128)(2,1)S(1)}, u32[]{:S(2)}, u32[]{:S(2)}) collective-permute-start(bf16[2,480,128]{2,1,0:T(8,128)(2,1)S(1)} %get-tuple-element.22), channel_id=1, source_target_pairs={{0,1},{1,0},{2,3},{3,2},{4,5},{5,4},{6,7},{7,6},{8,9},{9,8},{10,11... | collective-permute-start | bytes 737288 | tf_op jit(solution)/shard_map/ppermute | solution.py:447
  15.6 14.0 %collective-permute-start.2 = (bf16[1,480,128]{2,1,0:T(8,128)(2,1)S(1)}, bf16[1,480,128]{2,1,0:T(8,128)(2,1)S(1)}, u32[]{:S(2)}, u32[]{:S(2)}) collective-permute-start(bf16[1,480,128]{2,1,0:T(8,128)(2,1)S(1)} %get-tuple-element.27), channel_id=1, source_target_pairs={{0,1},{1,0},{2,3},{3,2},{4,5},{5,4},{6,7},{7,6},{8,9},{9,8},{10,11... | collective-permute-start | bytes 368648 | tf_op jit(solution)/shard_map/ppermute | solution.py:447
  17.8 13.8 %collective-permute-start = (bf16[1,480,128]{2,1,0:T(8,128)(2,1)S(1)}, bf16[1,480,128]{2,1,0:T(8,128)(2,1)S(1)}, u32[]{:S(2)}, u32[]{:S(2)}) collective-permute-start(bf16[1,480,128]{2,1,0:T(8,128)(2,1)S(1)} %get-tuple-element.21), channel_id=1, source_target_pairs={{0,1},{1,0},{2,3},{3,2},{4,5},{5,4},{6,7},{7,6},{8,9},{9,8},{10,11... | collective-permute-start | bytes 368648 | tf_op jit(solution)/shard_map/ppermute | solution.py:447
